TPU v7x, 128 devices: a whole 4x4x4 slice. The times are simulated.
128 devices in a mesh: heads: 8 (over y, core), tokens: 8 (over x_hi, z), cols: 2 (over x_lo).
Axes of the slice: x: 4 (x_hi: 2, x_lo: 2; x = x_hi * 2 + x_lo), y: 4, z: 4, core: 2. Of those that a mesh axis runs over, the one named last changes fastest.
Arguments:
- query_in: bfloat16 [4096, 8192], P('tokens', ('heads', 'cols')), may hold values from -24 to 24
- key_in: bfloat16 [4096, 8192], P('tokens', ('heads', 'cols')), may hold values from -24 to 24
- value_in: bfloat16 [4096, 8192], P('tokens', ('heads', 'cols')), may hold values from -6 to 6
- out_grads: bfloat16 [4096, 8192], P('tokens', ('heads', 'cols')), may hold values from -6 to 6
- doc_starts: int32 [6], replicated, may hold values from 0 to 4095, as said below
Outputs:
- input_factor: float32 [8192, 8192], P('heads', ('tokens', 'cols'))
- grad_factor: float32 [8192, 8192], P('heads', ('tokens', 'cols'))
Inputs may be any that keep to these rules, and one draw needn't show every extreme that they name: Strictly increasing with the first entry 0; document d runs from doc_starts[d] to the next start (the last one to 4096) - 1. One document holds (8 // 2 + 1) * 512 tokens.
All inputs are finite; a program needn't handle non-finite values.
Results may differ from a plain program's by a relative error of at most 0.0041.
Values may be sent and summed in bfloat16 or wider, within the bound.
No kernel may reach another device: no remote copies, remote signals or barrier semaphores. Data moves between devices by JAX's collectives and lax.ppermute only.
A program may use at most 128 MiB of HBM per device.

v0:
```python
import functools
import math

import jax
import jax.numpy as jnp
from jax import lax
from jax.experimental import pallas as pl
from jax.experimental.pallas import tpu as pltpu
from jax.sharding import Mesh
from jax.sharding import PartitionSpec as P

HEAD_DIM = 128
X = ("xh", "xl")
RING = (0, 3, 1, 2)
MASK_FLOOR = -1e30
KEY_STEP = 512
QUERY_STEP = 512
VMEM_BYTES = 56 * 1024 * 1024


def attention_kernel(starts, where_ref, *refs):
    kv_own, kv_oth, qg = refs[:4], refs[4:8], refs[8:12]
    att_ref, near_ref, far_ref = refs[12:15]
    k_all, v_all, q_ref, g_ref, v_turned, scores, grads, sems = refs[15:]
    half = q_ref.shape[0]
    part = half // 4
    half_id, z = where_ref[0], where_ref[1]
    own_at = pl.multiple_of(half_id * half, half)
    oth_at = pl.multiple_of((1 - half_id) * half, half)
    copies = []
    for pieces, base, targets in (
        (kv_own, own_at, (k_all, v_all)), (kv_oth, oth_at, (k_all, v_all)), (qg, 0, (q_ref, g_ref))
    ):
        for step, piece in zip(RING, pieces):
            at = pl.multiple_of(base + ((z + step) % 4) * part, part)
            for n, target in enumerate(targets):
                copies.append(
                    pltpu.make_async_copy(
                        piece.at[pl.ds(n * part, part)], target.at[pl.ds(at, part)], sems.at[len(copies)]
                    )
                )
    for copy in copies:
        copy.start()
    grads[...] = jnp.zeros_like(grads)
    for copy in copies:
        copy.wait()
    all_tokens = 2 * half
    docs = starts.shape[0]
    for at in range(0, all_tokens, KEY_STEP):
        v_turned[:, at : at + KEY_STEP] = v_all[at : at + KEY_STEP, :].T
    scale = math.log2(math.e) / math.sqrt(HEAD_DIM)
    groups = KEY_STEP // 8

    def query_block(block, carry):
        row = pl.multiple_of(block * QUERY_STEP, QUERY_STEP)
        first = own_at + row
        last = first + QUERY_STEP - 1
        pos = first + lax.broadcasted_iota(jnp.int32, (1, QUERY_STEP), 1)
        begin = jnp.zeros((1, QUERY_STEP), jnp.int32)
        finish = jnp.full((1, QUERY_STEP), all_tokens, jnp.int32)
        lowest, latest = jnp.int32(0), jnp.int32(0)
        highest, soonest = jnp.int32(all_tokens), jnp.int32(all_tokens)
        for d in range(docs):
            start = starts[d]
            lowest = jnp.where(start <= first, jnp.maximum(lowest, start), lowest)
            highest = jnp.where(start > last, jnp.minimum(highest, start), highest)
            latest = jnp.where(start <= last, jnp.maximum(latest, start), latest)
            soonest = jnp.where(start > first, jnp.minimum(soonest, start), soonest)
            begin = jnp.where(start <= pos, jnp.maximum(begin, start), begin)
            finish = jnp.where(start > pos, jnp.minimum(finish, start), finish)
        step_from = lowest // KEY_STEP
        step_to = (highest + KEY_STEP - 1) // KEY_STEP
        inside_from = jnp.minimum((latest + KEY_STEP - 1) // KEY_STEP, step_to)
        inside_to = jnp.maximum(soonest // KEY_STEP, inside_from)
        queries = q_ref[pl.ds(row, QUERY_STEP), :]
        cotangents = g_ref[pl.ds(row, QUERY_STEP), :]
        key_iota = lax.broadcasted_iota(jnp.int32, (KEY_STEP, QUERY_STEP), 0)

        def score_step(step, peak, masked):
            at = pl.multiple_of(step * KEY_STEP, KEY_STEP)
            s = lax.dot_general(
                k_all[pl.ds(at, KEY_STEP), :], queries, (((1,), (1,)), ((), ())),
                preferred_element_type=jnp.float32,
            ) * scale
            if masked:
                allowed = (key_iota >= begin - at) & (key_iota < finish - at)
                s = jnp.where(allowed, s, MASK_FLOOR)
            scores[pl.ds(at, KEY_STEP), :] = s
            return jnp.maximum(peak, jnp.max(s.reshape(groups, 8, QUERY_STEP), axis=0))

        edge_step = functools.partial(score_step, masked=True)
        inside_step = functools.partial(score_step, masked=False)
        peak = jnp.full((8, QUERY_STEP), MASK_FLOOR, jnp.float32)
        peak = lax.fori_loop(step_from, inside_from, edge_step, peak)
        peak = lax.fori_loop(inside_from, inside_to, inside_step, peak)
        peak = lax.fori_loop(inside_to, step_to, edge_step, peak)
        peak = jnp.max(peak, axis=0, keepdims=True)

        def mass_step(step, mass):
            at = pl.multiple_of(step * KEY_STEP, KEY_STEP)
            e = jnp.exp2(scores[pl.ds(at, KEY_STEP), :] - peak)
            scores[pl.ds(at, KEY_STEP), :] = e
            return mass + jnp.sum(e.reshape(groups, 8, QUERY_STEP), axis=0)

        mass = lax.fori_loop(step_from, step_to, mass_step, jnp.zeros((8, QUERY_STEP), jnp.float32))
        share = 1.0 / jnp.sum(mass, axis=0, keepdims=True)

        def value_step(step, summed):
            at = pl.multiple_of(step * KEY_STEP, KEY_STEP)
            w = (scores[pl.ds(at, KEY_STEP), :] * share).astype(jnp.bfloat16)
            grads[pl.ds(at, KEY_STEP), :] += jnp.dot(
                w, cotangents, preferred_element_type=jnp.float32
            )
            return summed + jnp.dot(
                v_turned[:, pl.ds(at, KEY_STEP)], w, preferred_element_type=jnp.float32
            )

        summed = lax.fori_loop(
            step_from, step_to, value_step, jnp.zeros((HEAD_DIM, QUERY_STEP), jnp.float32)
        )
        att_ref[:, pl.ds(row, QUERY_STEP)] = summed.astype(jnp.bfloat16)
        return carry

    lax.fori_loop(0, half // QUERY_STEP, query_block, 0)
    for at in range(0, half, KEY_STEP):
        near_ref[:, at : at + KEY_STEP] = grads[pl.ds(own_at + at, KEY_STEP), :].T
        far_ref[:, at : at + KEY_STEP] = grads[pl.ds(oth_at + at, KEY_STEP), :].T.astype(jnp.bfloat16)


def attention(starts, where, kv_own, kv_oth, qg):
    half = 2 * qg[0].shape[0]
    hbm = pl.BlockSpec(memory_space=pl.ANY)
    vmem = pl.BlockSpec(memory_space=pltpu.VMEM)
    smem = pl.BlockSpec(memory_space=pltpu.SMEM)
    return pl.pallas_call(
        attention_kernel,
        out_shape=(
            jax.ShapeDtypeStruct((HEAD_DIM, half), jnp.bfloat16),
            jax.ShapeDtypeStruct((HEAD_DIM, half), jnp.float32),
            jax.ShapeDtypeStruct((HEAD_DIM, half), jnp.bfloat16),
        ),
        in_specs=[smem, smem] + [hbm] * 12,
        out_specs=(vmem, vmem, vmem),
        scratch_shapes=[
            pltpu.VMEM((2 * half, HEAD_DIM), jnp.bfloat16),
            pltpu.VMEM((2 * half, HEAD_DIM), jnp.bfloat16),
            pltpu.VMEM((half, HEAD_DIM), jnp.bfloat16),
            pltpu.VMEM((half, HEAD_DIM), jnp.bfloat16),
            pltpu.VMEM((HEAD_DIM, 2 * half), jnp.bfloat16),
            pltpu.VMEM((2 * half, QUERY_STEP), jnp.float32),
            pltpu.VMEM((2 * half, HEAD_DIM), jnp.float32),
            pltpu.SemaphoreType.DMA((24,)),
        ],
        compiler_params=pltpu.CompilerParams(vmem_limit_bytes=VMEM_BYTES),
        name="attention",
    )(starts, where, *kv_own, *kv_oth, *qg)


def shifted(x, axis, by):
    count = lax.axis_size(axis)
    return lax.ppermute(x, axis, [(i, (i + by) % count) for i in range(count)])


def near_ring(x, axis):
    return shifted(x, axis, 1), shifted(x, axis, -1)


def heads_kernel(z_ref, *refs):
    sources, outs, sems = refs[:2], refs[2:6], refs[6]
    rows = sources[0].shape[0]
    copies = []
    for k, out in enumerate(outs):
        head = (z_ref[0] + k) % 4
        for n, source in enumerate(sources):
            copies.append(
                pltpu.make_async_copy(
                    source.at[:, pl.ds(pl.multiple_of(head * HEAD_DIM, HEAD_DIM), HEAD_DIM)],
                    out.at[pl.ds(n * rows, rows)], sems.at[len(copies)],
                )
            )
    for copy in copies:
        copy.start()
    for copy in copies:
        copy.wait()


def by_head(z, first, second):
    rows = first.shape[0]
    shape = jax.ShapeDtypeStruct((2 * rows, HEAD_DIM), first.dtype)
    hbm = pl.BlockSpec(memory_space=pl.ANY)
    vmem = pl.BlockSpec(memory_space=pltpu.VMEM)
    return pl.pallas_call(
        heads_kernel,
        out_shape=(shape,) * 4,
        in_specs=[pl.BlockSpec(memory_space=pltpu.SMEM), hbm, hbm],
        out_specs=(vmem,) * 4,
        scratch_shapes=[pltpu.SemaphoreType.DMA((8,))],
        name="by_head",
    )(z, first, second)


def swap_heads(parts):
    return parts[0], shifted(parts[1], "z", 1), shifted(parts[3], "z", -1), shifted(parts[2], "z", 2)


def stack_kernel(*refs):
    out, at = refs[-1], 0
    for part in refs[:-1]:
        out[at : at + part.shape[0], :] = part[...]
        at += part.shape[0]


def stacked(parts):
    rows = sum(p.shape[0] for p in parts)
    vmem = pl.BlockSpec(memory_space=pltpu.VMEM)
    return pl.pallas_call(
        stack_kernel,
        out_shape=jax.ShapeDtypeStruct((rows, *parts[0].shape[1:]), parts[0].dtype),
        in_specs=[vmem] * len(parts),
        out_specs=vmem,
        name="stack",
    )(*parts)


def factors_kernel(place, *refs, count, jobs, aliased):
    n_in = sum(job[0] + 1 for job in jobs)
    refs = list(refs)
    inputs, refs = refs[:n_in], refs[n_in + 2 * aliased :]
    outs, scratch = refs[: len(jobs)], refs[len(jobs) :]
    x, z = place[0], place[1]
    block = HEAD_DIM
    line = 8 - (x // 2) * 2 - z // 2 - 2 * (z % 2)
    waits, out_rows = [], []
    for j, (n_pieces, plan, _) in enumerate(jobs):
        rows, cols, sems = scratch[4 * j], scratch[4 * j + 1], scratch[4 * j + 3]
        pieces, col_ref = inputs[:n_pieces], inputs[n_pieces]
        inputs = inputs[n_pieces + 1 :]
        copies = []
        for n in range(8):
            at = pl.multiple_of(((n // 2 + line) % 4) * block, block)
            copies.append((col_ref.at[pl.ds(n * block, block)], cols.at[n % 2, pl.ds(at, block)]))
        targets, to = plan(x, z)
        for piece, pair in zip(pieces, targets):
            for n, (which, local) in enumerate(pair):
                at = pl.multiple_of(local * block, block)
                copies.append((piece.at[pl.ds(n * block, block)], rows.at[which, pl.ds(at, block)]))
        waits.append([pltpu.make_async_copy(src, dst, sems.at[k]) for k, (src, dst) in enumerate(copies)])
        out_rows.append(to)
        for copy in waits[-1]:
            copy.start()
    stores = []
    for j, (_, _, blocks) in enumerate(jobs):
        rows, cols, result, sems = scratch[4 * j : 4 * j + 4]
        for copy in waits[j]:
            copy.wait()
        total = None
        for which in range(2):
            part = lax.dot_general(
                rows[which], cols[which], (((1,), (1,)), ((), ())), preferred_element_type=jnp.float32
            )
            total = part if total is None else total + part
        result[...] = total * (1.0 / count)
        for local in range(blocks):
            row = pl.multiple_of(out_rows[j][local] * block, block)
            store = pltpu.make_async_copy(
                result.at[pl.ds(local * block, block)], outs[j].at[pl.ds(row, block)], sems.at[24 + local]
            )
            store.start()
            stores.append(store)
    for store in stores:
        store.wait()


def along_x_pieces(pieces):
    def plan(x, z):
        targets = [[((x + RING[outer]) % 4 // 2, slot) for slot in slots] for outer, slots in pieces]
        cols_at = (x + RING[pieces[0][0]]) % 2
        return targets, [cols_at * 4 + (z + RING[slot]) % 4 for slot in range(4)]

    return plan, 4


def along_z_pieces(pieces):
    groups = list(dict.fromkeys(outer for outer, _ in pieces))

    def plan(x, z):
        targets = []
        for outer, slots in pieces:
            at = [(x + RING[slot]) % 4 for slot in slots]
            targets.append([(xx // 2, groups.index(outer) * 2 + xx % 2) for xx in at])
        return targets, [c * 4 + (z + RING[g]) % 4 for g in groups for c in range(2)]

    return plan, 2 * len(groups)


def halved(groups):
    return [(outer, slots, groups[outer][n]) for outer in range(4) for n, slots in enumerate(((0, 1), (2, 3)))]


def factors_part(place, jobs, count, name, into=()):
    args, plans, scratch = [place], [], []
    for pieces, outers, cols, layout in jobs:
        held = [piece for piece in pieces if piece[0] in outers]
        plan, blocks = layout([(outer, slots) for outer, slots, _ in held])
        args += [array for _, _, array in held] + [cols]
        plans.append((len(held), plan, blocks))
        scratch += [
            pltpu.VMEM((2, blocks * HEAD_DIM, cols.shape[1]), jnp.bfloat16),
            pltpu.VMEM((2, 4 * HEAD_DIM, cols.shape[1]), jnp.bfloat16),
            pltpu.VMEM((blocks * HEAD_DIM, 4 * HEAD_DIM), jnp.float32),
            pltpu.SemaphoreType.DMA((32,)),
        ]
    hbm = pl.BlockSpec(memory_space=pl.ANY)
    aliased = len(into) > 0
    kernel = functools.partial(factors_kernel, count=count, jobs=plans, aliased=int(aliased))
    shape = jax.ShapeDtypeStruct((8 * HEAD_DIM, 4 * HEAD_DIM), jnp.float32)
    return pl.pallas_call(
        kernel,
        out_shape=(shape, shape),
        in_specs=[pl.BlockSpec(memory_space=pltpu.SMEM)] + [hbm] * (len(args) + len(into) - 1),
        out_specs=(hbm, hbm),
        input_output_aliases={len(args): 0, len(args) + 1: 1} if aliased else {},
        scratch_shapes=scratch,
        compiler_params=pltpu.CompilerParams(vmem_limit_bytes=VMEM_BYTES),
        name=name,
    )(*args, *into)


def column_moves():
    ranks = [(y, core, xh, z) for y in range(4) for core in range(2) for xh in range(2) for z in range(4)]
    place = {rank: n for n, rank in enumerate(ranks)}
    along_y, in_plane = [], []
    for y, core, xh, z in ranks:
        spread = (y + z + 2 * core) % 4
        along_y.append((place[y, core, xh, z], place[spread, core, xh, z]))
        in_plane.append((place[spread, core, xh, z], place[spread, xh, y // 2, (y % 2) * 2 + core]))
    return along_y, in_plane


def on_device(query_in, key_in, value_in, out_grads, doc_starts):
    all_tokens = query_in.shape[0] * 8
    xh, z = lax.axis_index("xh"), lax.axis_index("z")
    place = jnp.stack([lax.axis_index(X), z]).astype(jnp.int32)
    z_only = z.astype(jnp.int32)[None]
    kv_parts = by_head(z_only, key_in, value_in)
    kv_parts, query_in, out_grads = lax.optimization_barrier((kv_parts, query_in, out_grads))
    kv_own = swap_heads(kv_parts)
    kv_oth = tuple(shifted(piece, "xh", 1) for piece in kv_own)
    qg = swap_heads(by_head(z_only, query_in, out_grads))
    where = jnp.stack([xh, z]).astype(jnp.int32)
    attended, near, far = attention(doc_starts, where, kv_own, kv_oth, qg)
    line = ("y", "core", "xh", "z")
    along_y, in_plane = column_moves()
    far = shifted(far, "xh", 1)
    a_near = near_ring(attended, "z")
    a_col = lax.ppermute(attended, line, along_y)
    value_grads = (near + far).astype(jnp.bfloat16)
    g_near = near_ring(value_grads, X)
    g_far = shifted(value_grads, X, 2)
    g_col = lax.ppermute(lax.ppermute(value_grads, line, along_y), line, in_plane)
    a_far = shifted(attended, "z", 2)
    a_col = lax.ppermute(a_col, line, in_plane)
    a_first, a_second = stacked((attended, a_near[0])), stacked((a_near[1], a_far))
    g_first, g_second = stacked((value_grads, g_near[0])), stacked((g_near[1], g_far))
    a_first, a_second, a_col, g_first, g_second, g_col = lax.optimization_barrier(
        (a_first, a_second, a_col, g_first, g_second, g_col)
    )
    cols_a = lax.all_gather(a_col, ("y", "core"), axis=0, tiled=True)
    cols_g = lax.all_gather(g_col, ("y", "core"), axis=0, tiled=True)
    a_firsts, g_firsts = near_ring(a_first, X), near_ring(g_first, "z")
    a_firsts, g_firsts, a_second, g_second = lax.optimization_barrier((a_firsts, g_firsts, a_second, g_second))
    a_seconds, g_seconds = near_ring(a_second, X), near_ring(g_second, "z")
    a_firsts, g_firsts, a_seconds, g_seconds = lax.optimization_barrier((a_firsts, g_firsts, a_seconds, g_seconds))
    a_far = shifted(a_firsts[0], X, 1), shifted(a_seconds[1], X, -1)
    g_far = shifted(g_firsts[0], "z", 1), shifted(g_seconds[1], "z", -1)
    rows_a = halved(((a_first, a_second), *zip(a_firsts, a_seconds), a_far))
    rows_g = halved(((g_first, g_second), *zip(g_firsts, g_seconds), g_far))
    near = ((rows_a, (1, 2), cols_a, along_x_pieces), (rows_g, (0, 1, 2), cols_g, along_z_pieces))
    far = ((rows_a, (0, 3), cols_a, along_x_pieces), (rows_g, (3,), cols_g, along_z_pieces))
    factors = factors_part(place, near, all_tokens, "near_rows")
    return factors_part(place, far, all_tokens, "far_rows", factors)


def solution(mesh):
    split = Mesh(mesh.devices.reshape(4, 2, 2, 4, 2), ("y", "core", "xh", "z", "xl"))
    tokens, features = ("xh", "z"), ("y", "core", "xl")
    spec = P(tokens, features)
    out = P(("y", "core"), ("xh", "z", "xl"))
    return jax.shard_map(
        on_device, mesh=split, in_specs=(spec, spec, spec, spec, P()), out_specs=(out, out),
        check_vma=False,
    )
```

profile of v0, /device:TPU:24, one launch (start us, length us, event | category | flops | bytes accessed | tf_op | source)
XLA Modules:
  0.0 234.7 jit_solution(10922672827759349250)
XLA Ops:
  15.6 3.0 %collective-permute-start.3 = (bf16[1024,128]{1,0:T(8,128)(2,1)}, bf16[1024,128]{1,0:T(8,128)(2,1)S(1)}, u32[]{:S(2)}, u32[]{:S(2)}) collective-permute-start(bf16[1024,128]{1,0:T(8,128)(2,1)} %get-tuple-element.45.refs_0_), channel_id=1, source_target_pairs={{0,8},{8,0},{1,9},{9,1},{2,10},{10,2},{3,11},{11,3},{4,12},{12,4},... | collective-permute-start | bytes 786440 | tf_op jit(solution)/shard_map/ppermute | solution.py:161
  28.2 3.0 %collective-permute-start.4 = (bf16[1024,128]{1,0:T(8,128)(2,1)S(1)}, bf16[1024,128]{1,0:T(8,128)(2,1)S(1)}, u32[]{:S(2)}, u32[]{:S(2)}) collective-permute-start(bf16[1024,128]{1,0:T(8,128)(2,1)S(1)} %collective-permute-done.refs_1_), channel_id=1, source_target_pairs={{0,8},{8,0},{1,9},{9,1},{2,10},{10,2},{3,11},{11,3},{4,12},{12,4},... | collective-permute-start | bytes 786440 | tf_op jit(solution)/shard_map/ppermute | solution.py:161
  38.9 5.2 %collective-permute-done.5.refs_6_ = bf16[1024,128]{1,0:T(8,128)(2,1)S(1)} collective-permute-done((bf16[1024,128]{1,0:T(8,128)(2,1)S(1)}, bf16[1024,128]{1,0:T(8,128)(2,1)S(1)}, u32[]{:S(2)}, u32[]{:S(2)}) %collective-permute-start.5) | collective-permute-done | bytes 262176 | tf_op jit(solution)/shard_map/ppermute | solution.py:161
  44.1 2.8 %collective-permute-done.6.refs_7_ = bf16[1024,128]{1,0:T(8,128)(2,1)S(1)} collective-permute-done((bf16[1024,128]{1,0:T(8,128)(2,1)S(1)}, bf16[1024,128]{1,0:T(8,128)(2,1)S(1)}, u32[]{:S(2)}, u32[]{:S(2)}) %collective-permute-start.6) | collective-permute-done | bytes 262176 | tf_op jit(solution)/shard_map/ppermute | solution.py:161
  47.6 16.4 %attention.1 = (bf16[128,2048]{1,0:T(8,128)(2,1)}, f32[128,2048]{1,0:T(8,128)}, bf16[128,2048]{1,0:T(8,128)(2,1)}) custom-call(s32[6]{0:T(128)} %starts.1, s32[2]{0:T(128)} %pad_add_fusion.1.where_ref, bf16[1024,128]{1,0:T(8,128)(2,1)} %get-tuple-element.45.refs_0_, bf16[1024,128]{1,0:T(8,128)(2,1)} %copy-done.14, bf16[1024,128]{1,0:T(8,128)(2,1)} %copy-done.15, ...), custom_call_target="tpu_custom_call" | custom-call | tf_op jit(solution)/shard_map/attention/pallas_call | solution.py:135
  64.1 8.7 %collective-permute-start.15 = (bf16[128,2048]{1,0:T(8,128)(2,1)}, bf16[128,2048]{1,0:T(8,128)(2,1)S(1)}, u32[]{:S(2)}, u32[]{:S(2)}) collective-permute-start(bf16[128,2048]{1,0:T(8,128)(2,1)} %get-tuple-element.57), channel_id=1, source_target_pairs={{0,8},{8,0},{1,9},{9,1},{2,10},{10,2},{3,11},{11,3},{4,12},{12,4},... | collective-permute-start | bytes 1572872 | tf_op jit(solution)/shard_map/ppermute | solution.py:161
  72.8 5.4 %collective-permute-start.13 = (bf16[128,2048]{1,0:T(8,128)(2,1)}, bf16[128,2048]{1,0:T(8,128)(2,1)}, u32[]{:S(2)}, u32[]{:S(2)}) collective-permute-start(bf16[128,2048]{1,0:T(8,128)(2,1)} %get-tuple-element.55.refs_0_), channel_id=1, source_target_pairs={{0,0},{2,34},{4,68},{6,102},{8,8},{10,42},{12,76},{14,110},{16,80}... | collective-permute-start | bytes 1572872 | tf_op jit(solution)/shard_map/ppermute | solution.py:356
  84.1 5.4 %collective-permute-start.19 = (bf16[128,2048]{1,0:T(8,128)(2,1)}, bf16[128,2048]{1,0:T(8,128)(2,1)}, u32[]{:S(2)}, u32[]{:S(2)}) collective-permute-start(bf16[128,2048]{1,0:T(8,128)(2,1)} %add_convert_fusion.refs_0_), channel_id=1, source_target_pairs={{0,0},{2,34},{4,68},{6,102},{8,8},{10,42},{12,76},{14,110},{16,80}... | collective-permute-start | bytes 1572872 | tf_op jit(solution)/shard_map/ppermute | solution.py:360
  89.5 3.2 %collective-permute-start.18 = (bf16[128,2048]{1,0:T(8,128)(2,1)}, bf16[128,2048]{1,0:T(8,128)(2,1)}, u32[]{:S(2)}, u32[]{:S(2)}) collective-permute-start(bf16[128,2048]{1,0:T(8,128)(2,1)} %add_convert_fusion.refs_0_), channel_id=1, source_target_pairs={{0,8},{1,9},{8,0},{9,1},{2,10},{3,11},{10,2},{11,3},{4,12},{5,13},... | collective-permute-start | bytes 1572872 | tf_op jit(solution)/shard_map/ppermute | solution.py:161
  99.1 4.8 %collective-permute-start.14 = (bf16[128,2048]{1,0:T(8,128)(2,1)}, bf16[128,2048]{1,0:T(8,128)(2,1)}, u32[]{:S(2)}, u32[]{:S(2)}) collective-permute-start(bf16[128,2048]{1,0:T(8,128)(2,1)} %collective-permute-done.13), channel_id=1, source_target_pairs={{0,0},{34,32},{68,64},{102,96},{8,16},{42,48},{76,80},{110,112},{8... | collective-permute-start | bytes 1572872 | tf_op jit(solution)/shard_map/ppermute | solution.py:362
  103.9 4.9 %collective-permute-start.20 = (bf16[128,2048]{1,0:T(8,128)(2,1)}, bf16[128,2048]{1,0:T(8,128)(2,1)}, u32[]{:S(2)}, u32[]{:S(2)}) collective-permute-start(bf16[128,2048]{1,0:T(8,128)(2,1)} %collective-permute-done.19), channel_id=1, source_target_pairs={{0,0},{34,32},{68,64},{102,96},{8,16},{42,48},{76,80},{110,112},{8... | collective-permute-start | bytes 1572872 | tf_op jit(solution)/shard_map/ppermute | solution.py:360
  122.9 5.6 %collective-permute-done.20 = bf16[128,2048]{1,0:T(8,128)(2,1)} collective-permute-done((bf16[128,2048]{1,0:T(8,128)(2,1)}, bf16[128,2048]{1,0:T(8,128)(2,1)}, u32[]{:S(2)}, u32[]{:S(2)}) %collective-permute-start.20) | collective-permute-done | bytes 524320 | tf_op jit(solution)/shard_map/ppermute | solution.py:360
  134.6 18.3 %collective-permute-done.22.refs_2_ = bf16[256,2048]{1,0:T(8,128)(2,1)S(1)} collective-permute-done((bf16[256,2048]{1,0:T(8,128)(2,1)S(1)}, bf16[256,2048]{1,0:T(8,128)(2,1)S(1)}, u32[]{:S(2)}, u32[]{:S(2)}) %collective-permute-start.22) | collective-permute-done | bytes 1048608 | tf_op jit(solution)/shard_map/ppermute | solution.py:161
  152.9 3.5 %collective-permute-done.21.refs_0_ = bf16[256,2048]{1,0:T(8,128)(2,1)} collective-permute-done((bf16[256,2048]{1,0:T(8,128)(2,1)S(1)}, bf16[256,2048]{1,0:T(8,128)(2,1)}, u32[]{:S(2)}, u32[]{:S(2)}) %collective-permute-start.21) | collective-permute-done | bytes 1048608 | tf_op jit(solution)/shard_map/ppermute | solution.py:161
  158.5 3.0 %collective-permute-start.26 = (bf16[256,2048]{1,0:T(8,128)(2,1)S(1)}, bf16[256,2048]{1,0:T(8,128)(2,1)S(1)}, u32[]{:S(2)}, u32[]{:S(2)}) collective-permute-start(bf16[256,2048]{1,0:T(8,128)(2,1)S(1)} %copy-done.1), channel_id=1, source_target_pairs={{0,9},{1,0},{8,1},{9,8},{2,11},{3,2},{10,3},{11,10},{4,13},{5,4},{... | collective-permute-start | bytes 3145736 | tf_op jit(solution)/shard_map/ppermute | solution.py:161
  163.4 17.9 %collective-permute-done.26.refs_3_ = bf16[256,2048]{1,0:T(8,128)(2,1)S(1)} collective-permute-done((bf16[256,2048]{1,0:T(8,128)(2,1)S(1)}, bf16[256,2048]{1,0:T(8,128)(2,1)S(1)}, u32[]{:S(2)}, u32[]{:S(2)}) %collective-permute-start.26) | collective-permute-done | bytes 1048608 | tf_op jit(solution)/shard_map/ppermute | solution.py:161
  181.3 3.4 %collective-permute-done.25.refs_1_ = bf16[256,2048]{1,0:T(8,128)(2,1)S(1)} collective-permute-done((bf16[256,2048]{1,0:T(8,128)(2,1)S(1)}, bf16[256,2048]{1,0:T(8,128)(2,1)S(1)}, u32[]{:S(2)}, u32[]{:S(2)}) %collective-permute-start.25) | collective-permute-done | bytes 1048608 | tf_op jit(solution)/shard_map/ppermute | solution.py:161
  185.7 3.3 %collective-permute-done.27.refs_8_ = bf16[256,2048]{1,0:T(8,128)(2,1)S(1)} collective-permute-done((bf16[256,2048]{1,0:T(8,128)(2,1)}, bf16[256,2048]{1,0:T(8,128)(2,1)S(1)}, u32[]{:S(2)}, u32[]{:S(2)}) %collective-permute-start.27) | collective-permute-done | bytes 1048608 | tf_op jit(solution)/shard_map/ppermute | solution.py:161
  189.0 3.2 %collective-permute-start.30 = (bf16[256,2048]{1,0:T(8,128)(2,1)S(1)}, bf16[256,2048]{1,0:T(8,128)(2,1)}, u32[]{:S(2)}, u32[]{:S(2)}) collective-permute-start(bf16[256,2048]{1,0:T(8,128)(2,1)S(1)} %collective-permute-done.26.refs_3_), channel_id=1, source_target_pairs={{0,9},{1,0},{8,1},{9,8},{2,11},{3,2},{10,3},{11,10},{4,13},{5,4},{... | collective-permute-start | bytes 3145736 | tf_op jit(solution)/shard_map/ppermute | solution.py:161
  192.2 3.2 %collective-permute-start.32 = (bf16[256,2048]{1,0:T(8,128)(2,1)S(1)}, bf16[256,2048]{1,0:T(8,128)(2,1)}, u32[]{:S(2)}, u32[]{:S(2)}) collective-permute-start(bf16[256,2048]{1,0:T(8,128)(2,1)S(1)} %collective-permute-done.28.refs_10_), channel_id=1, source_target_pairs={{0,6},{2,0},{4,2},{6,4},{1,7},{3,1},{5,3},{7,5},{8,14},{10,8},{12,... | collective-permute-start | bytes 3145736 | tf_op jit(solution)/shard_map/ppermute | solution.py:161
  196.1 14.3 %near_rows.1 = (f32[1024,512]{1,0:T(8,128)}, f32[1024,512]{1,0:T(8,128)}) custom-call(s32[2]{0:T(128)} %pad_add_fusion.place, bf16[256,2048]{1,0:T(8,128)(2,1)} %collective-permute-done.21.refs_0_, bf16[256,2048]{1,0:T(8,128)(2,1)} %copy-done.8, bf16[256,2048]{1,0:T(8,128)(2,1)} %copy-done.3, bf16[256,2048]{1,0:T(8,128)(2,1)} %copy-done.5, ...), custom_call_target="tpu_custom_call" | custom-call | tf_op jit(solution)/shard_map/near_rows/pallas_call | solution.py:317
  210.4 4.1 %collective-permute-done.29.refs_2_ = bf16[256,2048]{1,0:T(8,128)(2,1)S(1)} collective-permute-done((bf16[256,2048]{1,0:T(8,128)(2,1)}, bf16[256,2048]{1,0:T(8,128)(2,1)S(1)}, u32[]{:S(2)}, u32[]{:S(2)}) %collective-permute-start.29) | collective-permute-done | bytes 1048608 | tf_op jit(solution)/shard_map/ppermute | solution.py:161
  214.5 2.8 %collective-permute-done.31.refs_5_ = bf16[256,2048]{1,0:T(8,128)(2,1)} collective-permute-done((bf16[256,2048]{1,0:T(8,128)(2,1)}, bf16[256,2048]{1,0:T(8,128)(2,1)}, u32[]{:S(2)}, u32[]{:S(2)}) %collective-permute-start.31) | collective-permute-done | bytes 1048608 | tf_op jit(solution)/shard_map/ppermute | solution.py:161
  217.3 10.6 %far_rows.1 = (f32[1024,512]{1,0:T(8,128)}, f32[1024,512]{1,0:T(8,128)}) custom-call(s32[2]{0:T(128)} %pad_add_fusion.place, bf16[256,2048]{1,0:T(8,128)(2,1)} %stack.25.refs_0_, bf16[256,2048]{1,0:T(8,128)(2,1)} %stack.26.refs_1_, bf16[256,2048]{1,0:T(8,128)(2,1)} %copy-done.7, ...), custom_call_target="tpu_custom_call", output_to_operand_aliasing={{0}: (9, {}), {1}: (10, {})} | custom-call | tf_op jit(solution)/shard_map/far_rows/pallas_call | solution.py:317
  (108 shorter events, 64.4 us)
Async XLA Ops:
  7.2 188.9 %all-gather.3.cloned.1.call-start = ((), (), s32[]{:S(2)}) async-start(), calls=%async_computation | async-start | bytes 4718592 | tf_op jit(solution)/shard_map/all_gather | solution.py:368
  64.1 17.9 %collective-permute-start.15 = (bf16[128,2048]{1,0:T(8,128)(2,1)}, bf16[128,2048]{1,0:T(8,128)(2,1)S(1)}, u32[]{:S(2)}, u32[]{:S(2)}) collective-permute-start(bf16[128,2048]{1,0:T(8,128)(2,1)} %get-tuple-element.57), channel_id=1, source_target_pairs={{0,8},{8,0},{1,9},{9,1},{2,10},{10,2},{3,11},{11,3},{4,12},{12,4},... | collective-permute-start | bytes 1572872 | tf_op jit(solution)/shard_map/ppermute | solution.py:161
  72.8 16.7 %collective-permute-start.13 = (bf16[128,2048]{1,0:T(8,128)(2,1)}, bf16[128,2048]{1,0:T(8,128)(2,1)}, u32[]{:S(2)}, u32[]{:S(2)}) collective-permute-start(bf16[128,2048]{1,0:T(8,128)(2,1)} %get-tuple-element.55.refs_0_), channel_id=1, source_target_pairs={{0,0},{2,34},{4,68},{6,102},{8,8},{10,42},{12,76},{14,110},{16,80}... | collective-permute-start | bytes 1572872 | tf_op jit(solution)/shard_map/ppermute | solution.py:356
  78.2 17.7 %collective-permute-start.11 = (bf16[128,2048]{1,0:T(8,128)(2,1)}, bf16[128,2048]{1,0:T(8,128)(2,1)S(1)}, u32[]{:S(2)}, u32[]{:S(2)}) collective-permute-start(bf16[128,2048]{1,0:T(8,128)(2,1)} %get-tuple-element.55.refs_0_), channel_id=1, source_target_pairs={{0,6},{2,0},{4,2},{6,4},{1,7},{3,1},{5,3},{7,5},{8,14},{10,8},{12,... | collective-permute-start | bytes 1572872 | tf_op jit(solution)/shard_map/ppermute | solution.py:161
  78.5 20.6 %collective-permute-start.10 = (bf16[128,2048]{1,0:T(8,128)(2,1)}, bf16[128,2048]{1,0:T(8,128)(2,1)S(1)}, u32[]{:S(2)}, u32[]{:S(2)}) collective-permute-start(bf16[128,2048]{1,0:T(8,128)(2,1)} %get-tuple-element.55.refs_0_), channel_id=1, source_target_pairs={{0,2},{2,4},{4,6},{6,0},{1,3},{3,5},{5,7},{7,1},{8,10},{10,12},{12... | collective-permute-start | bytes 1572872 | tf_op jit(solution)/shard_map/ppermute | solution.py:161
  84.1 19.8 %collective-permute-start.19 = (bf16[128,2048]{1,0:T(8,128)(2,1)}, bf16[128,2048]{1,0:T(8,128)(2,1)}, u32[]{:S(2)}, u32[]{:S(2)}) collective-permute-start(bf16[128,2048]{1,0:T(8,128)(2,1)} %add_convert_fusion.refs_0_), channel_id=1, source_target_pairs={{0,0},{2,34},{4,68},{6,102},{8,8},{10,42},{12,76},{14,110},{16,80}... | collective-permute-start | bytes 1572872 | tf_op jit(solution)/shard_map/ppermute | solution.py:360
  89.5 29.5 %collective-permute-start.18 = (bf16[128,2048]{1,0:T(8,128)(2,1)}, bf16[128,2048]{1,0:T(8,128)(2,1)}, u32[]{:S(2)}, u32[]{:S(2)}) collective-permute-start(bf16[128,2048]{1,0:T(8,128)(2,1)} %add_convert_fusion.refs_0_), channel_id=1, source_target_pairs={{0,8},{1,9},{8,0},{9,1},{2,10},{3,11},{10,2},{11,3},{4,12},{5,13},... | collective-permute-start | bytes 1572872 | tf_op jit(solution)/shard_map/ppermute | solution.py:161
  93.6 22.3 %collective-permute-start.16 = (bf16[128,2048]{1,0:T(8,128)(2,1)}, bf16[128,2048]{1,0:T(8,128)(2,1)S(1)}, u32[]{:S(2)}, u32[]{:S(2)}) collective-permute-start(bf16[128,2048]{1,0:T(8,128)(2,1)} %add_convert_fusion.refs_0_), channel_id=1, source_target_pairs={{0,1},{1,8},{8,9},{9,0},{2,3},{3,10},{10,11},{11,2},{4,5},{5,12},{... | collective-permute-start | bytes 1572872 | tf_op jit(solution)/shard_map/ppermute | solution.py:161
  95.9 23.1 %collective-permute-start.17 = (bf16[128,2048]{1,0:T(8,128)(2,1)}, bf16[128,2048]{1,0:T(8,128)(2,1)}, u32[]{:S(2)}, u32[]{:S(2)}) collective-permute-start(bf16[128,2048]{1,0:T(8,128)(2,1)} %add_convert_fusion.refs_0_), channel_id=1, source_target_pairs={{0,9},{1,0},{8,1},{9,8},{2,11},{3,2},{10,3},{11,10},{4,13},{5,4},{... | collective-permute-start | bytes 1572872 | tf_op jit(solution)/shard_map/ppermute | solution.py:161
  99.1 23.8 %collective-permute-start.14 = (bf16[128,2048]{1,0:T(8,128)(2,1)}, bf16[128,2048]{1,0:T(8,128)(2,1)}, u32[]{:S(2)}, u32[]{:S(2)}) collective-permute-start(bf16[128,2048]{1,0:T(8,128)(2,1)} %collective-permute-done.13), channel_id=1, source_target_pairs={{0,0},{34,32},{68,64},{102,96},{8,16},{42,48},{76,80},{110,112},{8... | collective-permute-start | bytes 1572872 | tf_op jit(solution)/shard_map/ppermute | solution.py:362
  103.9 24.6 %collective-permute-start.20 = (bf16[128,2048]{1,0:T(8,128)(2,1)}, bf16[128,2048]{1,0:T(8,128)(2,1)}, u32[]{:S(2)}, u32[]{:S(2)}) collective-permute-start(bf16[128,2048]{1,0:T(8,128)(2,1)} %collective-permute-done.19), channel_id=1, source_target_pairs={{0,0},{34,32},{68,64},{102,96},{8,16},{42,48},{76,80},{110,112},{8... | collective-permute-start | bytes 1572872 | tf_op jit(solution)/shard_map/ppermute | solution.py:360
  128.6 67.5 %all-gather.5.cloned.1.call-start = ((), (), s32[]{:S(2)}) async-start(), calls=%async_computation.1 | async-start | bytes 4718592 | tf_op jit(solution)/shard_map/all_gather | solution.py:369
  129.3 23.5 %collective-permute-start.22 = (bf16[256,2048]{1,0:T(8,128)(2,1)S(1)}, bf16[256,2048]{1,0:T(8,128)(2,1)S(1)}, u32[]{:S(2)}, u32[]{:S(2)}) collective-permute-start(bf16[256,2048]{1,0:T(8,128)(2,1)S(1)} %copy-done), channel_id=1, source_target_pairs={{0,9},{1,0},{8,1},{9,8},{2,11},{3,2},{10,3},{11,10},{4,13},{5,4},{... | collective-permute-start | bytes 3145736 | tf_op jit(solution)/shard_map/ppermute | solution.py:161
  131.2 25.2 %collective-permute-start.21 = (bf16[256,2048]{1,0:T(8,128)(2,1)S(1)}, bf16[256,2048]{1,0:T(8,128)(2,1)}, u32[]{:S(2)}, u32[]{:S(2)}) collective-permute-start(bf16[256,2048]{1,0:T(8,128)(2,1)S(1)} %copy-done), channel_id=1, source_target_pairs={{0,1},{1,8},{8,9},{9,0},{2,3},{3,10},{10,11},{11,2},{4,5},{5,12},{... | collective-permute-start | bytes 3145736 | tf_op jit(solution)/shard_map/ppermute | solution.py:161
  132.6 23.8 %collective-permute-start.24 = (bf16[256,2048]{1,0:T(8,128)(2,1)S(1)}, bf16[256,2048]{1,0:T(8,128)(2,1)S(1)}, u32[]{:S(2)}, u32[]{:S(2)}) collective-permute-start(bf16[256,2048]{1,0:T(8,128)(2,1)S(1)} %copy-done.2), channel_id=1, source_target_pairs={{0,6},{2,0},{4,2},{6,4},{1,7},{3,1},{5,3},{7,5},{8,14},{10,8},{12,... | collective-permute-start | bytes 3145736 | tf_op jit(solution)/shard_map/ppermute | solution.py:161
  133.6 24.9 %collective-permute-start.23 = (bf16[256,2048]{1,0:T(8,128)(2,1)S(1)}, bf16[256,2048]{1,0:T(8,128)(2,1)}, u32[]{:S(2)}, u32[]{:S(2)}) collective-permute-start(bf16[256,2048]{1,0:T(8,128)(2,1)S(1)} %copy-done.2), channel_id=1, source_target_pairs={{0,2},{2,4},{4,6},{6,0},{1,3},{3,5},{5,7},{7,1},{8,10},{10,12},{12... | collective-permute-start | bytes 3145736 | tf_op jit(solution)/shard_map/ppermute | solution.py:161
  158.5 22.8 %collective-permute-start.26 = (bf16[256,2048]{1,0:T(8,128)(2,1)S(1)}, bf16[256,2048]{1,0:T(8,128)(2,1)S(1)}, u32[]{:S(2)}, u32[]{:S(2)}) collective-permute-start(bf16[256,2048]{1,0:T(8,128)(2,1)S(1)} %copy-done.1), channel_id=1, source_target_pairs={{0,9},{1,0},{8,1},{9,8},{2,11},{3,2},{10,3},{11,10},{4,13},{5,4},{... | collective-permute-start | bytes 3145736 | tf_op jit(solution)/shard_map/ppermute | solution.py:161
  161.4 23.3 %collective-permute-start.25 = (bf16[256,2048]{1,0:T(8,128)(2,1)S(1)}, bf16[256,2048]{1,0:T(8,128)(2,1)S(1)}, u32[]{:S(2)}, u32[]{:S(2)}) collective-permute-start(bf16[256,2048]{1,0:T(8,128)(2,1)S(1)} %copy-done.1), channel_id=1, source_target_pairs={{0,1},{1,8},{8,9},{9,0},{2,3},{3,10},{10,11},{11,2},{4,5},{5,12},{... | collective-permute-start | bytes 3145736 | tf_op jit(solution)/shard_map/ppermute | solution.py:161
  161.4 24.3 %collective-permute-start.28 = (bf16[256,2048]{1,0:T(8,128)(2,1)}, bf16[256,2048]{1,0:T(8,128)(2,1)S(1)}, u32[]{:S(2)}, u32[]{:S(2)}) collective-permute-start(bf16[256,2048]{1,0:T(8,128)(2,1)} %stack.28.refs_6_), channel_id=1, source_target_pairs={{0,6},{2,0},{4,2},{6,4},{1,7},{3,1},{5,3},{7,5},{8,14},{10,8},{12,... | collective-permute-start | bytes 3145736 | tf_op jit(solution)/shard_map/ppermute | solution.py:161
  162.7 26.3 %collective-permute-start.27 = (bf16[256,2048]{1,0:T(8,128)(2,1)}, bf16[256,2048]{1,0:T(8,128)(2,1)S(1)}, u32[]{:S(2)}, u32[]{:S(2)}) collective-permute-start(bf16[256,2048]{1,0:T(8,128)(2,1)} %stack.28.refs_6_), channel_id=1, source_target_pairs={{0,2},{2,4},{4,6},{6,0},{1,3},{3,5},{5,7},{7,1},{8,10},{10,12},{12... | collective-permute-start | bytes 3145736 | tf_op jit(solution)/shard_map/ppermute | solution.py:161
  189.0 25.5 %collective-permute-start.29 = (bf16[256,2048]{1,0:T(8,128)(2,1)}, bf16[256,2048]{1,0:T(8,128)(2,1)S(1)}, u32[]{:S(2)}, u32[]{:S(2)}) collective-permute-start(bf16[256,2048]{1,0:T(8,128)(2,1)} %collective-permute-done.21.refs_0_), channel_id=1, source_target_pairs={{0,1},{1,8},{8,9},{9,0},{2,3},{3,10},{10,11},{11,2},{4,5},{5,12},{... | collective-permute-start | bytes 3145736 | tf_op jit(solution)/shard_map/ppermute | solution.py:161
  189.0 25.5 %collective-permute-start.30 = (bf16[256,2048]{1,0:T(8,128)(2,1)S(1)}, bf16[256,2048]{1,0:T(8,128)(2,1)}, u32[]{:S(2)}, u32[]{:S(2)}) collective-permute-start(bf16[256,2048]{1,0:T(8,128)(2,1)S(1)} %collective-permute-done.26.refs_3_), channel_id=1, source_target_pairs={{0,9},{1,0},{8,1},{9,8},{2,11},{3,2},{10,3},{11,10},{4,13},{5,4},{... | collective-permute-start | bytes 3145736 | tf_op jit(solution)/shard_map/ppermute | solution.py:161
  192.2 25.0 %collective-permute-start.31 = (bf16[256,2048]{1,0:T(8,128)(2,1)}, bf16[256,2048]{1,0:T(8,128)(2,1)}, u32[]{:S(2)}, u32[]{:S(2)}) collective-permute-start(bf16[256,2048]{1,0:T(8,128)(2,1)} %collective-permute-done.23.refs_7_), channel_id=1, source_target_pairs={{0,2},{2,4},{4,6},{6,0},{1,3},{3,5},{5,7},{7,1},{8,10},{10,12},{12... | collective-permute-start | bytes 3145736 | tf_op jit(solution)/shard_map/ppermute | solution.py:161
  192.2 25.0 %collective-permute-start.32 = (bf16[256,2048]{1,0:T(8,128)(2,1)S(1)}, bf16[256,2048]{1,0:T(8,128)(2,1)}, u32[]{:S(2)}, u32[]{:S(2)}) collective-permute-start(bf16[256,2048]{1,0:T(8,128)(2,1)S(1)} %collective-permute-done.28.refs_10_), channel_id=1, source_target_pairs={{0,6},{2,0},{4,2},{6,4},{1,7},{3,1},{5,3},{7,5},{8,14},{10,8},{12,... | collective-permute-start | bytes 3145736 | tf_op jit(solution)/shard_map/ppermute | solution.py:161
  (35 other events, 479.9 us)
Sparse Core Ops, SparseCore 0:
  128.7 30.3 all-gather.2
  160.8 32.0 all-gather.4
where the time goes:
time: 239 us; the launch traced here: 235 us
  waiting for transfers between devices  87.3 us (37%)
  starting transfers between devices  73.1 us (31%)
  Pallas kernels  55.2 us (23%)
  between operations  14.3 us (6%)
  other arithmetic  3.31 us (1%)
    ppermute x29, waiting for transfers between devices, shifted(): return lax.ppermute(x, axis, [(i, (i + by) % count) for i in range(count)])  79.5 us
    ppermute x29, starting transfers between devices, shifted(): return lax.ppermute(x, axis, [(i, (i + by) % count) for i in range(count)])  52.6 us
    pallas_call x2, Pallas kernels, factors_part(): pl.pallas_call(kernel, out_shape=(shape, shape), in_specs=[pl.BlockSpec(m...  24.9 us
    pallas_call x1, Pallas kernels, attention(): pl.pallas_call(attention_kernel, out_shape=(jax.ShapeDtypeStruct((HEAD_DI...  16.4 us
    pallas_call x4, Pallas kernels, stacked(): pl.pallas_call(stack_kernel, out_shape=jax.ShapeDtypeStruct((rows, *parts...  9.13 us
    ppermute x1, waiting for transfers between devices, on_device(): lax.ppermute(lax.ppermute(value_grads, line, along_y), line, in_plane)  5.62 us
    ppermute x1, starting transfers between devices, on_device(): a_col = lax.ppermute(attended, line, along_y)  5.38 us
    ppermute x1, starting transfers between devices, on_device(): lax.ppermute(value_grads, line, along_y)  5.37 us
  transfers between devices with their start and end apart: 35, of which 24 were waited for; matrix products, arithmetic and copies ran while one was open for 1% of the time, Pallas kernels for 11%

commit v1 on v0

--- a/solution.py
+++ b/solution.py
@@ -343,8 +343,9 @@
     place = jnp.stack([lax.axis_index(X), z]).astype(jnp.int32)
     z_only = z.astype(jnp.int32)[None]
     kv_parts = by_head(z_only, key_in, value_in)
-    kv_parts, query_in, out_grads = lax.optimization_barrier((kv_parts, query_in, out_grads))
-    kv_own = swap_heads(kv_parts)
+    own, below, above, across = swap_heads(kv_parts)
+    below, above, query_in, out_grads = lax.optimization_barrier((below, above, query_in, out_grads))
+    kv_own = (own, below, above, across)
     kv_oth = tuple(shifted(piece, "xh", 1) for piece in kv_own)
     qg = swap_heads(by_head(z_only, query_in, out_grads))
     where = jnp.stack([xh, z]).astype(jnp.int32)

time: 239 us -> 233 us (0.975)
  starting transfers between devices: 73.1 us -> 61.5 us
  Pallas kernels: 55.2 us -> 63.8 us
    ppermute x29, starting transfers between devices: 52.6 us -> 41.4 us  [shifted(): return lax.ppermute(x, axis, [(i, (i + by) % count) for i in range(count)])]
    pallas_call x1, Pallas kernels: 16.4 us -> 25.1 us  [attention(): pl.pallas_call(attention_kernel, out_shape=(jax.ShapeDtypeStruct((HEAD_DI...]
    ppermute x1, starting transfers between devices: 4.86 us -> 1.92 us  [on_device(): lax.ppermute(lax.ppermute(value_grads, line, along_y), line, in_plane)]
    ppermute x1, starting transfers between devices: 4.81 us -> 7.34 us  [on_device(): a_col = lax.ppermute(a_col, line, in_plane)]
  transfers between devices with their start and end apart: 35 -> 35, of which waited for: 24 -> 19; matrix products, arithmetic and copies ran while one was open for 1% -> 1% of each run, Pallas kernels for 11% -> 11%
where the time goes in v1:
time: 233 us; the launch traced here: 230 us
  waiting for transfers between devices  85.9 us (37%)
  Pallas kernels  63.8 us (27%)
  starting transfers between devices  61.5 us (26%)
  between operations  14.3 us (6%)
  other arithmetic  3.31 us (1%)
    ppermute x29, waiting for transfers between devices, shifted(): return lax.ppermute(x, axis, [(i, (i + by) % count) for i in range(count)])  77.2 us
    ppermute x29, starting transfers between devices, shifted(): return lax.ppermute(x, axis, [(i, (i + by) % count) for i in range(count)])  41.4 us
    pallas_call x1, Pallas kernels, attention(): pl.pallas_call(attention_kernel, out_shape=(jax.ShapeDtypeStruct((HEAD_DI...  25.1 us
    pallas_call x2, Pallas kernels, factors_part(): pl.pallas_call(kernel, out_shape=(shape, shape), in_specs=[pl.BlockSpec(m...  24.9 us
    pallas_call x4, Pallas kernels, stacked(): pl.pallas_call(stack_kernel, out_shape=jax.ShapeDtypeStruct((rows, *parts...  9.13 us
    ppermute x1, starting transfers between devices, on_device(): a_col = lax.ppermute(a_col, line, in_plane)  7.34 us
    ppermute x1, waiting for transfers between devices, on_device(): lax.ppermute(lax.ppermute(value_grads, line, along_y), line, in_plane)  5.62 us
    ppermute x1, starting transfers between devices, on_device(): a_col = lax.ppermute(attended, line, along_y)  5.38 us
  transfers between devices with their start and end apart: 35, of which 19 were waited for; matrix products, arithmetic and copies ran while one was open for 1% of the time, Pallas kernels for 11%

profile of v1, /device:TPU:24, one launch (start us, length us, event | category | flops | bytes accessed | tf_op | source)
XLA Modules:
  0.0 230.3 jit_solution(14870029409981227975)
XLA Ops:
  15.5 3.0 %collective-permute-start.3 = (bf16[1024,128]{1,0:T(8,128)(2,1)}, bf16[1024,128]{1,0:T(8,128)(2,1)S(1)}, u32[]{:S(2)}, u32[]{:S(2)}) collective-permute-start(bf16[1024,128]{1,0:T(8,128)(2,1)} %get-tuple-element.39.refs_0_), channel_id=1, source_target_pairs={{0,8},{8,0},{1,9},{9,1},{2,10},{10,2},{3,11},{11,3},{4,12},{12,4},... | collective-permute-start | bytes 786440 | tf_op jit(solution)/shard_map/ppermute | solution.py:161
  20.2 5.1 %collective-permute-done.1.refs_2_ = bf16[1024,128]{1,0:T(8,128)(2,1)S(1)} collective-permute-done((bf16[1024,128]{1,0:T(8,128)(2,1)}, bf16[1024,128]{1,0:T(8,128)(2,1)S(1)}, u32[]{:S(2)}, u32[]{:S(2)}) %collective-permute-start.1) | collective-permute-done | bytes 262176 | tf_op jit(solution)/shard_map/ppermute | solution.py:161
  25.3 3.0 %collective-permute-start.4 = (bf16[1024,128]{1,0:T(8,128)(2,1)S(1)}, bf16[1024,128]{1,0:T(8,128)(2,1)S(1)}, u32[]{:S(2)}, u32[]{:S(2)}) collective-permute-start(bf16[1024,128]{1,0:T(8,128)(2,1)S(1)} %collective-permute-done.refs_1_), channel_id=1, source_target_pairs={{0,8},{8,0},{1,9},{9,1},{2,10},{10,2},{3,11},{11,3},{4,12},{12,4},... | collective-permute-start | bytes 786440 | tf_op jit(solution)/shard_map/ppermute | solution.py:161
  31.3 3.6 %collective-permute-start.8 = (bf16[1024,128]{1,0:T(8,128)(2,1)}, bf16[1024,128]{1,0:T(8,128)(2,1)S(1)}, u32[]{:S(2)}, u32[]{:S(2)}) collective-permute-start(bf16[1024,128]{1,0:T(8,128)(2,1)} %get-tuple-element.49), channel_id=1, source_target_pairs={{0,6},{2,0},{4,2},{6,4},{1,7},{3,1},{5,3},{7,5},{8,14},{10,8},{12,... | collective-permute-start | bytes 786440 | tf_op jit(solution)/shard_map/ppermute | solution.py:161
  34.9 3.0 %collective-permute-start.6 = (bf16[1024,128]{1,0:T(8,128)(2,1)S(1)}, bf16[1024,128]{1,0:T(8,128)(2,1)S(1)}, u32[]{:S(2)}, u32[]{:S(2)}) collective-permute-start(bf16[1024,128]{1,0:T(8,128)(2,1)S(1)} %collective-permute-done.2.refs_3_), channel_id=1, source_target_pairs={{0,8},{8,0},{1,9},{9,1},{2,10},{10,2},{3,11},{11,3},{4,12},{12,4},... | collective-permute-start | bytes 786440 | tf_op jit(solution)/shard_map/ppermute | solution.py:161
  40.0 2.8 %collective-permute-done.6.refs_7_ = bf16[1024,128]{1,0:T(8,128)(2,1)S(1)} collective-permute-done((bf16[1024,128]{1,0:T(8,128)(2,1)S(1)}, bf16[1024,128]{1,0:T(8,128)(2,1)S(1)}, u32[]{:S(2)}, u32[]{:S(2)}) %collective-permute-start.6) | collective-permute-done | bytes 262176 | tf_op jit(solution)/shard_map/ppermute | solution.py:161
  42.8 3.2 %collective-permute-done.9.refs_11_ = bf16[1024,128]{1,0:T(8,128)(2,1)S(1)} collective-permute-done((bf16[1024,128]{1,0:T(8,128)(2,1)}, bf16[1024,128]{1,0:T(8,128)(2,1)S(1)}, u32[]{:S(2)}, u32[]{:S(2)}) %collective-permute-start.9) | collective-permute-done | bytes 262176 | tf_op jit(solution)/shard_map/ppermute | solution.py:161
  46.7 25.1 %attention.1 = (bf16[128,2048]{1,0:T(8,128)(2,1)}, f32[128,2048]{1,0:T(8,128)}, bf16[128,2048]{1,0:T(8,128)(2,1)}) custom-call(s32[6]{0:T(128)} %starts.1, s32[2]{0:T(128)} %pad_add_fusion.1.where_ref, bf16[1024,128]{1,0:T(8,128)(2,1)} %get-tuple-element.39.refs_0_, bf16[1024,128]{1,0:T(8,128)(2,1)} %copy-done.14, bf16[1024,128]{1,0:T(8,128)(2,1)} %copy-done.15, ...), custom_call_target="tpu_custom_call" | custom-call | tf_op jit(solution)/shard_map/attention/pallas_call | solution.py:135
  72.5 5.4 %collective-permute-start.13 = (bf16[128,2048]{1,0:T(8,128)(2,1)}, bf16[128,2048]{1,0:T(8,128)(2,1)}, u32[]{:S(2)}, u32[]{:S(2)}) collective-permute-start(bf16[128,2048]{1,0:T(8,128)(2,1)} %get-tuple-element.51.refs_0_), channel_id=1, source_target_pairs={{0,0},{2,34},{4,68},{6,102},{8,8},{10,42},{12,76},{14,110},{16,80}... | collective-permute-start | bytes 1572872 | tf_op jit(solution)/shard_map/ppermute | solution.py:357
  79.9 2.9 %collective-permute-done.15 = bf16[128,2048]{1,0:T(8,128)(2,1)S(1)} collective-permute-done((bf16[128,2048]{1,0:T(8,128)(2,1)}, bf16[128,2048]{1,0:T(8,128)(2,1)S(1)}, u32[]{:S(2)}, u32[]{:S(2)}) %collective-permute-start.15) | collective-permute-done | bytes 524320 | tf_op jit(solution)/shard_map/ppermute | solution.py:161
  84.9 5.4 %collective-permute-start.19 = (bf16[128,2048]{1,0:T(8,128)(2,1)}, bf16[128,2048]{1,0:T(8,128)(2,1)}, u32[]{:S(2)}, u32[]{:S(2)}) collective-permute-start(bf16[128,2048]{1,0:T(8,128)(2,1)} %add_convert_fusion.refs_0_), channel_id=1, source_target_pairs={{0,0},{2,34},{4,68},{6,102},{8,8},{10,42},{12,76},{14,110},{16,80}... | collective-permute-start | bytes 1572872 | tf_op jit(solution)/shard_map/ppermute | solution.py:361
  97.5 7.3 %collective-permute-start.14 = (bf16[128,2048]{1,0:T(8,128)(2,1)}, bf16[128,2048]{1,0:T(8,128)(2,1)}, u32[]{:S(2)}, u32[]{:S(2)}) collective-permute-start(bf16[128,2048]{1,0:T(8,128)(2,1)} %collective-permute-done.13), channel_id=1, source_target_pairs={{0,0},{34,32},{68,64},{102,96},{8,16},{42,48},{76,80},{110,112},{8... | collective-permute-start | bytes 1572872 | tf_op jit(solution)/shard_map/ppermute | solution.py:363
  121.3 5.6 %collective-permute-done.20 = bf16[128,2048]{1,0:T(8,128)(2,1)} collective-permute-done((bf16[128,2048]{1,0:T(8,128)(2,1)}, bf16[128,2048]{1,0:T(8,128)(2,1)}, u32[]{:S(2)}, u32[]{:S(2)}) %collective-permute-start.20) | collective-permute-done | bytes 524320 | tf_op jit(solution)/shard_map/ppermute | solution.py:361
  132.0 19.0 %collective-permute-done.22.refs_2_ = bf16[256,2048]{1,0:T(8,128)(2,1)S(1)} collective-permute-done((bf16[256,2048]{1,0:T(8,128)(2,1)S(1)}, bf16[256,2048]{1,0:T(8,128)(2,1)S(1)}, u32[]{:S(2)}, u32[]{:S(2)}) %collective-permute-start.22) | collective-permute-done | bytes 1048608 | tf_op jit(solution)/shard_map/ppermute | solution.py:161
  151.0 3.5 %collective-permute-done.21.refs_0_ = bf16[256,2048]{1,0:T(8,128)(2,1)} collective-permute-done((bf16[256,2048]{1,0:T(8,128)(2,1)S(1)}, bf16[256,2048]{1,0:T(8,128)(2,1)}, u32[]{:S(2)}, u32[]{:S(2)}) %collective-permute-start.21) | collective-permute-done | bytes 1048608 | tf_op jit(solution)/shard_map/ppermute | solution.py:161
  155.9 3.0 %collective-permute-start.26 = (bf16[256,2048]{1,0:T(8,128)(2,1)S(1)}, bf16[256,2048]{1,0:T(8,128)(2,1)S(1)}, u32[]{:S(2)}, u32[]{:S(2)}) collective-permute-start(bf16[256,2048]{1,0:T(8,128)(2,1)S(1)} %copy-done.1), channel_id=1, source_target_pairs={{0,9},{1,0},{8,1},{9,8},{2,11},{3,2},{10,3},{11,10},{4,13},{5,4},{... | collective-permute-start | bytes 3145736 | tf_op jit(solution)/shard_map/ppermute | solution.py:161
  160.9 20.4 %collective-permute-done.26.refs_3_ = bf16[256,2048]{1,0:T(8,128)(2,1)S(1)} collective-permute-done((bf16[256,2048]{1,0:T(8,128)(2,1)S(1)}, bf16[256,2048]{1,0:T(8,128)(2,1)S(1)}, u32[]{:S(2)}, u32[]{:S(2)}) %collective-permute-start.26) | collective-permute-done | bytes 1048608 | tf_op jit(solution)/shard_map/ppermute | solution.py:161
  181.2 3.4 %collective-permute-done.25.refs_1_ = bf16[256,2048]{1,0:T(8,128)(2,1)S(1)} collective-permute-done((bf16[256,2048]{1,0:T(8,128)(2,1)S(1)}, bf16[256,2048]{1,0:T(8,128)(2,1)S(1)}, u32[]{:S(2)}, u32[]{:S(2)}) %collective-permute-start.25) | collective-permute-done | bytes 1048608 | tf_op jit(solution)/shard_map/ppermute | solution.py:161
  185.4 2.7 %collective-permute-start.30 = (bf16[256,2048]{1,0:T(8,128)(2,1)S(1)}, bf16[256,2048]{1,0:T(8,128)(2,1)}, u32[]{:S(2)}, u32[]{:S(2)}) collective-permute-start(bf16[256,2048]{1,0:T(8,128)(2,1)S(1)} %collective-permute-done.26.refs_3_), channel_id=1, source_target_pairs={{0,9},{1,0},{8,1},{9,8},{2,11},{3,2},{10,3},{11,10},{4,13},{5,4},{... | collective-permute-start | bytes 3145736 | tf_op jit(solution)/shard_map/ppermute | solution.py:161
  188.6 2.7 %collective-permute-start.32 = (bf16[256,2048]{1,0:T(8,128)(2,1)S(1)}, bf16[256,2048]{1,0:T(8,128)(2,1)}, u32[]{:S(2)}, u32[]{:S(2)}) collective-permute-start(bf16[256,2048]{1,0:T(8,128)(2,1)S(1)} %collective-permute-done.28.refs_10_), channel_id=1, source_target_pairs={{0,6},{2,0},{4,2},{6,4},{1,7},{3,1},{5,3},{7,5},{8,14},{10,8},{12,... | collective-permute-start | bytes 3145736 | tf_op jit(solution)/shard_map/ppermute | solution.py:161
  191.9 14.3 %near_rows.1 = (f32[1024,512]{1,0:T(8,128)}, f32[1024,512]{1,0:T(8,128)}) custom-call(s32[2]{0:T(128)} %pad_add_fusion.place, bf16[256,2048]{1,0:T(8,128)(2,1)} %collective-permute-done.21.refs_0_, bf16[256,2048]{1,0:T(8,128)(2,1)} %copy-done.8, bf16[256,2048]{1,0:T(8,128)(2,1)} %copy-done.3, bf16[256,2048]{1,0:T(8,128)(2,1)} %copy-done.5, ...), custom_call_target="tpu_custom_call" | custom-call | tf_op jit(solution)/shard_map/near_rows/pallas_call | solution.py:317
  206.3 3.8 %collective-permute-done.29.refs_2_ = bf16[256,2048]{1,0:T(8,128)(2,1)S(1)} collective-permute-done((bf16[256,2048]{1,0:T(8,128)(2,1)}, bf16[256,2048]{1,0:T(8,128)(2,1)S(1)}, u32[]{:S(2)}, u32[]{:S(2)}) %collective-permute-start.29) | collective-permute-done | bytes 1048608 | tf_op jit(solution)/shard_map/ppermute | solution.py:161
  210.1 2.8 %collective-permute-done.31.refs_5_ = bf16[256,2048]{1,0:T(8,128)(2,1)} collective-permute-done((bf16[256,2048]{1,0:T(8,128)(2,1)}, bf16[256,2048]{1,0:T(8,128)(2,1)}, u32[]{:S(2)}, u32[]{:S(2)}) %collective-permute-start.31) | collective-permute-done | bytes 1048608 | tf_op jit(solution)/shard_map/ppermute | solution.py:161
  212.8 10.6 %far_rows.1 = (f32[1024,512]{1,0:T(8,128)}, f32[1024,512]{1,0:T(8,128)}) custom-call(s32[2]{0:T(128)} %pad_add_fusion.place, bf16[256,2048]{1,0:T(8,128)(2,1)} %stack.25.refs_0_, bf16[256,2048]{1,0:T(8,128)(2,1)} %stack.26.refs_1_, bf16[256,2048]{1,0:T(8,128)(2,1)} %copy-done.7, ...), custom_call_target="tpu_custom_call", output_to_operand_aliasing={{0}: (9, {}), {1}: (10, {})} | custom-call | tf_op jit(solution)/shard_map/far_rows/pallas_call | solution.py:317
  (108 shorter events, 54.4 us)
Async XLA Ops:
  7.2 184.8 %all-gather.3.cloned.1.call-start = ((), (), s32[]{:S(2)}) async-start(), calls=%async_computation | async-start | bytes 4718592 | tf_op jit(solution)/shard_map/all_gather | solution.py:369
  13.8 17.5 %collective-permute-start.2 = (bf16[1024,128]{1,0:T(8,128)(2,1)}, bf16[1024,128]{1,0:T(8,128)(2,1)S(1)}, u32[]{:S(2)}, u32[]{:S(2)}) collective-permute-start(bf16[1024,128]{1,0:T(8,128)(2,1)} %get-tuple-element.44), channel_id=1, source_target_pairs={{0,4},{2,6},{4,0},{6,2},{1,5},{3,7},{5,1},{7,3},{8,12},{10,14},{12... | collective-permute-start | bytes 786440 | tf_op jit(solution)/shard_map/ppermute | solution.py:161
  15.5 19.4 %collective-permute-start.3 = (bf16[1024,128]{1,0:T(8,128)(2,1)}, bf16[1024,128]{1,0:T(8,128)(2,1)S(1)}, u32[]{:S(2)}, u32[]{:S(2)}) collective-permute-start(bf16[1024,128]{1,0:T(8,128)(2,1)} %get-tuple-element.39.refs_0_), channel_id=1, source_target_pairs={{0,8},{8,0},{1,9},{9,1},{2,10},{10,2},{3,11},{11,3},{4,12},{12,4},... | collective-permute-start | bytes 786440 | tf_op jit(solution)/shard_map/ppermute | solution.py:161
  72.5 17.8 %collective-permute-start.13 = (bf16[128,2048]{1,0:T(8,128)(2,1)}, bf16[128,2048]{1,0:T(8,128)(2,1)}, u32[]{:S(2)}, u32[]{:S(2)}) collective-permute-start(bf16[128,2048]{1,0:T(8,128)(2,1)} %get-tuple-element.51.refs_0_), channel_id=1, source_target_pairs={{0,0},{2,34},{4,68},{6,102},{8,8},{10,42},{12,76},{14,110},{16,80}... | collective-permute-start | bytes 1572872 | tf_op jit(solution)/shard_map/ppermute | solution.py:357
  79.1 18.4 %collective-permute-start.10 = (bf16[128,2048]{1,0:T(8,128)(2,1)}, bf16[128,2048]{1,0:T(8,128)(2,1)S(1)}, u32[]{:S(2)}, u32[]{:S(2)}) collective-permute-start(bf16[128,2048]{1,0:T(8,128)(2,1)} %get-tuple-element.51.refs_0_), channel_id=1, source_target_pairs={{0,2},{2,4},{4,6},{6,0},{1,3},{3,5},{5,7},{7,1},{8,10},{10,12},{12... | collective-permute-start | bytes 1572872 | tf_op jit(solution)/shard_map/ppermute | solution.py:161
  84.9 19.9 %collective-permute-start.19 = (bf16[128,2048]{1,0:T(8,128)(2,1)}, bf16[128,2048]{1,0:T(8,128)(2,1)}, u32[]{:S(2)}, u32[]{:S(2)}) collective-permute-start(bf16[128,2048]{1,0:T(8,128)(2,1)} %add_convert_fusion.refs_0_), channel_id=1, source_target_pairs={{0,0},{2,34},{4,68},{6,102},{8,8},{10,42},{12,76},{14,110},{16,80}... | collective-permute-start | bytes 1572872 | tf_op jit(solution)/shard_map/ppermute | solution.py:361
  90.3 26.2 %collective-permute-start.18 = (bf16[128,2048]{1,0:T(8,128)(2,1)}, bf16[128,2048]{1,0:T(8,128)(2,1)}, u32[]{:S(2)}, u32[]{:S(2)}) collective-permute-start(bf16[128,2048]{1,0:T(8,128)(2,1)} %add_convert_fusion.refs_0_), channel_id=1, source_target_pairs={{0,8},{1,9},{8,0},{9,1},{2,10},{3,11},{10,2},{11,3},{4,12},{5,13},... | collective-permute-start | bytes 1572872 | tf_op jit(solution)/shard_map/ppermute | solution.py:161
  92.0 21.4 %collective-permute-start.16 = (bf16[128,2048]{1,0:T(8,128)(2,1)}, bf16[128,2048]{1,0:T(8,128)(2,1)S(1)}, u32[]{:S(2)}, u32[]{:S(2)}) collective-permute-start(bf16[128,2048]{1,0:T(8,128)(2,1)} %add_convert_fusion.refs_0_), channel_id=1, source_target_pairs={{0,1},{1,8},{8,9},{9,0},{2,3},{3,10},{10,11},{11,2},{4,5},{5,12},{... | collective-permute-start | bytes 1572872 | tf_op jit(solution)/shard_map/ppermute | solution.py:161
  94.9 21.6 %collective-permute-start.17 = (bf16[128,2048]{1,0:T(8,128)(2,1)}, bf16[128,2048]{1,0:T(8,128)(2,1)}, u32[]{:S(2)}, u32[]{:S(2)}) collective-permute-start(bf16[128,2048]{1,0:T(8,128)(2,1)} %add_convert_fusion.refs_0_), channel_id=1, source_target_pairs={{0,9},{1,0},{8,1},{9,8},{2,11},{3,2},{10,3},{11,10},{4,13},{5,4},{... | collective-permute-start | bytes 1572872 | tf_op jit(solution)/shard_map/ppermute | solution.py:161
  97.5 23.8 %collective-permute-start.14 = (bf16[128,2048]{1,0:T(8,128)(2,1)}, bf16[128,2048]{1,0:T(8,128)(2,1)}, u32[]{:S(2)}, u32[]{:S(2)}) collective-permute-start(bf16[128,2048]{1,0:T(8,128)(2,1)} %collective-permute-done.13), channel_id=1, source_target_pairs={{0,0},{34,32},{68,64},{102,96},{8,16},{42,48},{76,80},{110,112},{8... | collective-permute-start | bytes 1572872 | tf_op jit(solution)/shard_map/ppermute | solution.py:363
  104.9 22.1 %collective-permute-start.20 = (bf16[128,2048]{1,0:T(8,128)(2,1)}, bf16[128,2048]{1,0:T(8,128)(2,1)}, u32[]{:S(2)}, u32[]{:S(2)}) collective-permute-start(bf16[128,2048]{1,0:T(8,128)(2,1)} %collective-permute-done.19), channel_id=1, source_target_pairs={{0,0},{34,32},{68,64},{102,96},{8,16},{42,48},{76,80},{110,112},{8... | collective-permute-start | bytes 1572872 | tf_op jit(solution)/shard_map/ppermute | solution.py:361
  127.0 65.0 %all-gather.5.cloned.1.call-start = ((), (), s32[]{:S(2)}) async-start(), calls=%async_computation.1 | async-start | bytes 4718592 | tf_op jit(solution)/shard_map/all_gather | solution.py:370
  127.7 23.3 %collective-permute-start.22 = (bf16[256,2048]{1,0:T(8,128)(2,1)S(1)}, bf16[256,2048]{1,0:T(8,128)(2,1)S(1)}, u32[]{:S(2)}, u32[]{:S(2)}) collective-permute-start(bf16[256,2048]{1,0:T(8,128)(2,1)S(1)} %copy-done), channel_id=1, source_target_pairs={{0,9},{1,0},{8,1},{9,8},{2,11},{3,2},{10,3},{11,10},{4,13},{5,4},{... | collective-permute-start | bytes 3145736 | tf_op jit(solution)/shard_map/ppermute | solution.py:161
  128.6 25.9 %collective-permute-start.21 = (bf16[256,2048]{1,0:T(8,128)(2,1)S(1)}, bf16[256,2048]{1,0:T(8,128)(2,1)}, u32[]{:S(2)}, u32[]{:S(2)}) collective-permute-start(bf16[256,2048]{1,0:T(8,128)(2,1)S(1)} %copy-done), channel_id=1, source_target_pairs={{0,1},{1,8},{8,9},{9,0},{2,3},{3,10},{10,11},{11,2},{4,5},{5,12},{... | collective-permute-start | bytes 3145736 | tf_op jit(solution)/shard_map/ppermute | solution.py:161
  130.0 24.5 %collective-permute-start.24 = (bf16[256,2048]{1,0:T(8,128)(2,1)S(1)}, bf16[256,2048]{1,0:T(8,128)(2,1)S(1)}, u32[]{:S(2)}, u32[]{:S(2)}) collective-permute-start(bf16[256,2048]{1,0:T(8,128)(2,1)S(1)} %copy-done.2), channel_id=1, source_target_pairs={{0,6},{2,0},{4,2},{6,4},{1,7},{3,1},{5,3},{7,5},{8,14},{10,8},{12,... | collective-permute-start | bytes 3145736 | tf_op jit(solution)/shard_map/ppermute | solution.py:161
  130.0 25.9 %collective-permute-start.23 = (bf16[256,2048]{1,0:T(8,128)(2,1)S(1)}, bf16[256,2048]{1,0:T(8,128)(2,1)}, u32[]{:S(2)}, u32[]{:S(2)}) collective-permute-start(bf16[256,2048]{1,0:T(8,128)(2,1)S(1)} %copy-done.2), channel_id=1, source_target_pairs={{0,2},{2,4},{4,6},{6,0},{1,3},{3,5},{5,7},{7,1},{8,10},{10,12},{12... | collective-permute-start | bytes 3145736 | tf_op jit(solution)/shard_map/ppermute | solution.py:161
  155.9 25.3 %collective-permute-start.26 = (bf16[256,2048]{1,0:T(8,128)(2,1)S(1)}, bf16[256,2048]{1,0:T(8,128)(2,1)S(1)}, u32[]{:S(2)}, u32[]{:S(2)}) collective-permute-start(bf16[256,2048]{1,0:T(8,128)(2,1)S(1)} %copy-done.1), channel_id=1, source_target_pairs={{0,9},{1,0},{8,1},{9,8},{2,11},{3,2},{10,3},{11,10},{4,13},{5,4},{... | collective-permute-start | bytes 3145736 | tf_op jit(solution)/shard_map/ppermute | solution.py:161
  158.8 25.8 %collective-permute-start.25 = (bf16[256,2048]{1,0:T(8,128)(2,1)S(1)}, bf16[256,2048]{1,0:T(8,128)(2,1)S(1)}, u32[]{:S(2)}, u32[]{:S(2)}) collective-permute-start(bf16[256,2048]{1,0:T(8,128)(2,1)S(1)} %copy-done.1), channel_id=1, source_target_pairs={{0,1},{1,8},{8,9},{9,0},{2,3},{3,10},{10,11},{11,2},{4,5},{5,12},{... | collective-permute-start | bytes 3145736 | tf_op jit(solution)/shard_map/ppermute | solution.py:161
  158.8 25.8 %collective-permute-start.28 = (bf16[256,2048]{1,0:T(8,128)(2,1)}, bf16[256,2048]{1,0:T(8,128)(2,1)S(1)}, u32[]{:S(2)}, u32[]{:S(2)}) collective-permute-start(bf16[256,2048]{1,0:T(8,128)(2,1)} %stack.28.refs_6_), channel_id=1, source_target_pairs={{0,6},{2,0},{4,2},{6,4},{1,7},{3,1},{5,3},{7,5},{8,14},{10,8},{12,... | collective-permute-start | bytes 3145736 | tf_op jit(solution)/shard_map/ppermute | solution.py:161
  158.8 26.0 %collective-permute-start.27 = (bf16[256,2048]{1,0:T(8,128)(2,1)}, bf16[256,2048]{1,0:T(8,128)(2,1)S(1)}, u32[]{:S(2)}, u32[]{:S(2)}) collective-permute-start(bf16[256,2048]{1,0:T(8,128)(2,1)} %stack.28.refs_6_), channel_id=1, source_target_pairs={{0,2},{2,4},{4,6},{6,0},{1,3},{3,5},{5,7},{7,1},{8,10},{10,12},{12... | collective-permute-start | bytes 3145736 | tf_op jit(solution)/shard_map/ppermute | solution.py:161
  184.9 25.2 %collective-permute-start.29 = (bf16[256,2048]{1,0:T(8,128)(2,1)}, bf16[256,2048]{1,0:T(8,128)(2,1)S(1)}, u32[]{:S(2)}, u32[]{:S(2)}) collective-permute-start(bf16[256,2048]{1,0:T(8,128)(2,1)} %collective-permute-done.21.refs_0_), channel_id=1, source_target_pairs={{0,1},{1,8},{8,9},{9,0},{2,3},{3,10},{10,11},{11,2},{4,5},{5,12},{... | collective-permute-start | bytes 3145736 | tf_op jit(solution)/shard_map/ppermute | solution.py:161
  185.4 24.7 %collective-permute-start.30 = (bf16[256,2048]{1,0:T(8,128)(2,1)S(1)}, bf16[256,2048]{1,0:T(8,128)(2,1)}, u32[]{:S(2)}, u32[]{:S(2)}) collective-permute-start(bf16[256,2048]{1,0:T(8,128)(2,1)S(1)} %collective-permute-done.26.refs_3_), channel_id=1, source_target_pairs={{0,9},{1,0},{8,1},{9,8},{2,11},{3,2},{10,3},{11,10},{4,13},{5,4},{... | collective-permute-start | bytes 3145736 | tf_op jit(solution)/shard_map/ppermute | solution.py:161
  188.1 24.7 %collective-permute-start.31 = (bf16[256,2048]{1,0:T(8,128)(2,1)}, bf16[256,2048]{1,0:T(8,128)(2,1)}, u32[]{:S(2)}, u32[]{:S(2)}) collective-permute-start(bf16[256,2048]{1,0:T(8,128)(2,1)} %collective-permute-done.23.refs_7_), channel_id=1, source_target_pairs={{0,2},{2,4},{4,6},{6,0},{1,3},{3,5},{5,7},{7,1},{8,10},{10,12},{12... | collective-permute-start | bytes 3145736 | tf_op jit(solution)/shard_map/ppermute | solution.py:161
  188.6 24.2 %collective-permute-start.32 = (bf16[256,2048]{1,0:T(8,128)(2,1)S(1)}, bf16[256,2048]{1,0:T(8,128)(2,1)}, u32[]{:S(2)}, u32[]{:S(2)}) collective-permute-start(bf16[256,2048]{1,0:T(8,128)(2,1)S(1)} %collective-permute-done.28.refs_10_), channel_id=1, source_target_pairs={{0,6},{2,0},{4,2},{6,4},{1,7},{3,1},{5,3},{7,5},{8,14},{10,8},{12,... | collective-permute-start | bytes 3145736 | tf_op jit(solution)/shard_map/ppermute | solution.py:161
  (35 other events, 424.3 us)
Sparse Core Ops, SparseCore 0:
  127.1 30.1 all-gather.2
  159.0 32.0 all-gather.4

commit v2 on v1

--- a/solution.py
+++ b/solution.py
@@ -359,7 +359,8 @@
     g_near = near_ring(value_grads, X)
     g_far = shifted(value_grads, X, 2)
     g_col = lax.ppermute(lax.ppermute(value_grads, line, along_y), line, in_plane)
-    a_far = shifted(attended, "z", 2)
+    tile, far = lax.optimization_barrier((attended, far))
+    a_far = shifted(tile, "z", 2)
     a_col = lax.ppermute(a_col, line, in_plane)
     a_first, a_second = stacked((attended, a_near[0])), stacked((a_near[1], a_far))
     g_first, g_second = stacked((value_grads, g_near[0])), stacked((g_near[1], g_far))

time: 233 us -> 235 us (level)
  the two profiles are of different devices: /device:TPU:24 before, /device:TPU:8 now
where the time goes in v2:
time: 235 us
  waiting for transfers between devices  82.9 us (35%)
  starting transfers between devices  70.3 us (30%)
  Pallas kernels  63.8 us (27%)
  between operations  14.3 us (6%)
  other arithmetic  2.58 us (1%)
    ppermute x29, waiting for transfers between devices, shifted(): return lax.ppermute(x, axis, [(i, (i + by) % count) for i in range(count)])  75 us
    ppermute x29, starting transfers between devices, shifted(): return lax.ppermute(x, axis, [(i, (i + by) % count) for i in range(count)])  49.3 us
    pallas_call x1, Pallas kernels, attention(): pl.pallas_call(attention_kernel, out_shape=(jax.ShapeDtypeStruct((HEAD_DI...  25 us
    pallas_call x2, Pallas kernels, factors_part(): pl.pallas_call(kernel, out_shape=(shape, shape), in_specs=[pl.BlockSpec(m...  24.9 us
    pallas_call x4, Pallas kernels, stacked(): pl.pallas_call(stack_kernel, out_shape=jax.ShapeDtypeStruct((rows, *parts...  9.18 us
    ppermute x1, starting transfers between devices, on_device(): lax.ppermute(lax.ppermute(value_grads, line, along_y), line, in_plane)  8.53 us
    ppermute x1, waiting for transfers between devices, on_device(): lax.ppermute(lax.ppermute(value_grads, line, along_y), line, in_plane)  5.62 us
    ppermute x1, starting transfers between devices, on_device(): a_col = lax.ppermute(a_col, line, in_plane)  5.59 us
  transfers between devices with their start and end apart: 35, of which 17 were waited for; matrix products, arithmetic and copies ran while one was open for 1% of the time, Pallas kernels for 11%

profile of v2, /device:TPU:8, one launch (start us, length us, event | category | flops | bytes accessed | tf_op | source)
XLA Modules:
  0.0 235.4 jit_solution(15671274845286495299)
XLA Ops:
  15.5 3.0 %collective-permute-start.3 = (bf16[1024,128]{1,0:T(8,128)(2,1)}, bf16[1024,128]{1,0:T(8,128)(2,1)S(1)}, u32[]{:S(2)}, u32[]{:S(2)}) collective-permute-start(bf16[1024,128]{1,0:T(8,128)(2,1)} %get-tuple-element.40.refs_0_), channel_id=1, source_target_pairs={{0,8},{8,0},{1,9},{9,1},{2,10},{10,2},{3,11},{11,3},{4,12},{12,4},... | collective-permute-start | bytes 786440 | tf_op jit(solution)/shard_map/ppermute | solution.py:161
  20.2 5.1 %collective-permute-done.1.refs_2_ = bf16[1024,128]{1,0:T(8,128)(2,1)S(1)} collective-permute-done((bf16[1024,128]{1,0:T(8,128)(2,1)}, bf16[1024,128]{1,0:T(8,128)(2,1)S(1)}, u32[]{:S(2)}, u32[]{:S(2)}) %collective-permute-start.1) | collective-permute-done | bytes 262176 | tf_op jit(solution)/shard_map/ppermute | solution.py:161
  25.3 3.0 %collective-permute-start.4 = (bf16[1024,128]{1,0:T(8,128)(2,1)S(1)}, bf16[1024,128]{1,0:T(8,128)(2,1)S(1)}, u32[]{:S(2)}, u32[]{:S(2)}) collective-permute-start(bf16[1024,128]{1,0:T(8,128)(2,1)S(1)} %collective-permute-done.refs_1_), channel_id=1, source_target_pairs={{0,8},{8,0},{1,9},{9,1},{2,10},{10,2},{3,11},{11,3},{4,12},{12,4},... | collective-permute-start | bytes 786440 | tf_op jit(solution)/shard_map/ppermute | solution.py:161
  31.3 3.6 %collective-permute-start.8 = (bf16[1024,128]{1,0:T(8,128)(2,1)}, bf16[1024,128]{1,0:T(8,128)(2,1)S(1)}, u32[]{:S(2)}, u32[]{:S(2)}) collective-permute-start(bf16[1024,128]{1,0:T(8,128)(2,1)} %get-tuple-element.50), channel_id=1, source_target_pairs={{0,6},{2,0},{4,2},{6,4},{1,7},{3,1},{5,3},{7,5},{8,14},{10,8},{12,... | collective-permute-start | bytes 786440 | tf_op jit(solution)/shard_map/ppermute | solution.py:161
  34.9 3.0 %collective-permute-start.6 = (bf16[1024,128]{1,0:T(8,128)(2,1)S(1)}, bf16[1024,128]{1,0:T(8,128)(2,1)S(1)}, u32[]{:S(2)}, u32[]{:S(2)}) collective-permute-start(bf16[1024,128]{1,0:T(8,128)(2,1)S(1)} %collective-permute-done.2.refs_3_), channel_id=1, source_target_pairs={{0,8},{8,0},{1,9},{9,1},{2,10},{10,2},{3,11},{11,3},{4,12},{12,4},... | collective-permute-start | bytes 786440 | tf_op jit(solution)/shard_map/ppermute | solution.py:161
  40.0 2.7 %collective-permute-done.6.refs_7_ = bf16[1024,128]{1,0:T(8,128)(2,1)S(1)} collective-permute-done((bf16[1024,128]{1,0:T(8,128)(2,1)S(1)}, bf16[1024,128]{1,0:T(8,128)(2,1)S(1)}, u32[]{:S(2)}, u32[]{:S(2)}) %collective-permute-start.6) | collective-permute-done | bytes 262176 | tf_op jit(solution)/shard_map/ppermute | solution.py:161
  42.8 3.2 %collective-permute-done.9.refs_11_ = bf16[1024,128]{1,0:T(8,128)(2,1)S(1)} collective-permute-done((bf16[1024,128]{1,0:T(8,128)(2,1)}, bf16[1024,128]{1,0:T(8,128)(2,1)S(1)}, u32[]{:S(2)}, u32[]{:S(2)}) %collective-permute-start.9) | collective-permute-done | bytes 262176 | tf_op jit(solution)/shard_map/ppermute | solution.py:161
  46.7 25.0 %attention.1 = (bf16[128,2048]{1,0:T(8,128)(2,1)}, f32[128,2048]{1,0:T(8,128)}, bf16[128,2048]{1,0:T(8,128)(2,1)}) custom-call(s32[6]{0:T(128)} %starts.1, s32[2]{0:T(128)} %pad_add_fusion.1.where_ref, bf16[1024,128]{1,0:T(8,128)(2,1)} %get-tuple-element.40.refs_0_, bf16[1024,128]{1,0:T(8,128)(2,1)} %copy-done.15, bf16[1024,128]{1,0:T(8,128)(2,1)} %copy-done.16, ...), custom_call_target="tpu_custom_call" | custom-call | tf_op jit(solution)/shard_map/attention/pallas_call | solution.py:135
  72.5 5.3 %collective-permute-start.14 = (bf16[128,2048]{1,0:T(8,128)(2,1)}, bf16[128,2048]{1,0:T(8,128)(2,1)}, u32[]{:S(2)}, u32[]{:S(2)}) collective-permute-start(bf16[128,2048]{1,0:T(8,128)(2,1)} %get-tuple-element.54.refs_0_), channel_id=1, source_target_pairs={{0,0},{2,34},{4,68},{6,102},{8,8},{10,42},{12,76},{14,110},{16,80}... | collective-permute-start | bytes 1572872 | tf_op jit(solution)/shard_map/ppermute | solution.py:357
  77.8 4.9 %collective-permute-done.12 = bf16[128,2048]{1,0:T(8,128)(2,1)S(1)} collective-permute-done((bf16[128,2048]{1,0:T(8,128)(2,1)}, bf16[128,2048]{1,0:T(8,128)(2,1)S(1)}, u32[]{:S(2)}, u32[]{:S(2)}) %collective-permute-start.12) | collective-permute-done | bytes 524320 | tf_op jit(solution)/shard_map/ppermute | solution.py:161
  87.5 4.0 %collective-permute-start.11 = (bf16[128,2048]{1,0:T(8,128)(2,1)}, bf16[128,2048]{1,0:T(8,128)(2,1)}, u32[]{:S(2)}, u32[]{:S(2)}) collective-permute-start(bf16[128,2048]{1,0:T(8,128)(2,1)} %get-tuple-element.54.refs_0_), channel_id=1, source_target_pairs={{0,6},{2,0},{4,2},{6,4},{1,7},{3,1},{5,3},{7,5},{8,14},{10,8},{12,... | collective-permute-start | bytes 1572872 | tf_op jit(solution)/shard_map/ppermute | solution.py:161
  94.2 4.0 %collective-permute-start.13 = (bf16[128,2048]{1,0:T(8,128)(2,1)}, bf16[128,2048]{1,0:T(8,128)(2,1)}, u32[]{:S(2)}, u32[]{:S(2)}) collective-permute-start(bf16[128,2048]{1,0:T(8,128)(2,1)} %get-tuple-element.54.refs_0_), channel_id=1, source_target_pairs={{0,4},{2,6},{4,0},{6,2},{1,5},{3,7},{5,1},{7,3},{8,12},{10,14},{12... | collective-permute-start | bytes 1572872 | tf_op jit(solution)/shard_map/ppermute | solution.py:161
  100.6 5.6 %collective-permute-start.15 = (bf16[128,2048]{1,0:T(8,128)(2,1)}, bf16[128,2048]{1,0:T(8,128)(2,1)}, u32[]{:S(2)}, u32[]{:S(2)}) collective-permute-start(bf16[128,2048]{1,0:T(8,128)(2,1)} %collective-permute-done.14), channel_id=1, source_target_pairs={{0,0},{34,32},{68,64},{102,96},{8,16},{42,48},{76,80},{110,112},{8... | collective-permute-start | bytes 1572872 | tf_op jit(solution)/shard_map/ppermute | solution.py:364
  106.2 8.5 %collective-permute-start.20 = (bf16[128,2048]{1,0:T(8,128)(2,1)}, bf16[128,2048]{1,0:T(8,128)(2,1)}, u32[]{:S(2)}, u32[]{:S(2)}) collective-permute-start(bf16[128,2048]{1,0:T(8,128)(2,1)} %collective-permute-done.19), channel_id=1, source_target_pairs={{0,0},{34,32},{68,64},{102,96},{8,16},{42,48},{76,80},{110,112},{8... | collective-permute-start | bytes 1572872 | tf_op jit(solution)/shard_map/ppermute | solution.py:361
  124.8 5.6 %collective-permute-done.20 = bf16[128,2048]{1,0:T(8,128)(2,1)} collective-permute-done((bf16[128,2048]{1,0:T(8,128)(2,1)}, bf16[128,2048]{1,0:T(8,128)(2,1)}, u32[]{:S(2)}, u32[]{:S(2)}) %collective-permute-start.20) | collective-permute-done | bytes 524320 | tf_op jit(solution)/shard_map/ppermute | solution.py:361
  135.3 18.5 %collective-permute-done.22.refs_2_ = bf16[256,2048]{1,0:T(8,128)(2,1)S(1)} collective-permute-done((bf16[256,2048]{1,0:T(8,128)(2,1)S(1)}, bf16[256,2048]{1,0:T(8,128)(2,1)S(1)}, u32[]{:S(2)}, u32[]{:S(2)}) %collective-permute-start.22) | collective-permute-done | bytes 1048608 | tf_op jit(solution)/shard_map/ppermute | solution.py:161
  153.8 4.3 %collective-permute-done.21.refs_0_ = bf16[256,2048]{1,0:T(8,128)(2,1)} collective-permute-done((bf16[256,2048]{1,0:T(8,128)(2,1)S(1)}, bf16[256,2048]{1,0:T(8,128)(2,1)}, u32[]{:S(2)}, u32[]{:S(2)}) %collective-permute-start.21) | collective-permute-done | bytes 1048608 | tf_op jit(solution)/shard_map/ppermute | solution.py:161
  163.4 20.9 %collective-permute-done.26.refs_3_ = bf16[256,2048]{1,0:T(8,128)(2,1)S(1)} collective-permute-done((bf16[256,2048]{1,0:T(8,128)(2,1)}, bf16[256,2048]{1,0:T(8,128)(2,1)S(1)}, u32[]{:S(2)}, u32[]{:S(2)}) %collective-permute-start.26) | collective-permute-done | bytes 1048608 | tf_op jit(solution)/shard_map/ppermute | solution.py:161
  189.2 3.0 %collective-permute-start.30 = (bf16[256,2048]{1,0:T(8,128)(2,1)S(1)}, bf16[256,2048]{1,0:T(8,128)(2,1)}, u32[]{:S(2)}, u32[]{:S(2)}) collective-permute-start(bf16[256,2048]{1,0:T(8,128)(2,1)S(1)} %collective-permute-done.26.refs_3_), channel_id=1, source_target_pairs={{0,9},{1,0},{8,1},{9,8},{2,11},{3,2},{10,3},{11,10},{4,13},{5,4},{... | collective-permute-start | bytes 3145736 | tf_op jit(solution)/shard_map/ppermute | solution.py:161
  192.3 3.1 %collective-permute-start.32 = (bf16[256,2048]{1,0:T(8,128)(2,1)S(1)}, bf16[256,2048]{1,0:T(8,128)(2,1)}, u32[]{:S(2)}, u32[]{:S(2)}) collective-permute-start(bf16[256,2048]{1,0:T(8,128)(2,1)S(1)} %collective-permute-done.28.refs_10_), channel_id=1, source_target_pairs={{0,6},{2,0},{4,2},{6,4},{1,7},{3,1},{5,3},{7,5},{8,14},{10,8},{12,... | collective-permute-start | bytes 3145736 | tf_op jit(solution)/shard_map/ppermute | solution.py:161
  197.5 14.3 %near_rows.1 = (f32[1024,512]{1,0:T(8,128)}, f32[1024,512]{1,0:T(8,128)}) custom-call(s32[2]{0:T(128)} %pad_add_fusion.place, bf16[256,2048]{1,0:T(8,128)(2,1)} %collective-permute-done.21.refs_0_, bf16[256,2048]{1,0:T(8,128)(2,1)} %copy-done.9, bf16[256,2048]{1,0:T(8,128)(2,1)} %copy-done.4, bf16[256,2048]{1,0:T(8,128)(2,1)} %copy-done.6, ...), custom_call_target="tpu_custom_call" | custom-call | tf_op jit(solution)/shard_map/near_rows/pallas_call | solution.py:317
  211.8 3.2 %collective-permute-done.29.refs_2_ = bf16[256,2048]{1,0:T(8,128)(2,1)S(1)} collective-permute-done((bf16[256,2048]{1,0:T(8,128)(2,1)}, bf16[256,2048]{1,0:T(8,128)(2,1)S(1)}, u32[]{:S(2)}, u32[]{:S(2)}) %collective-permute-start.29) | collective-permute-done | bytes 1048608 | tf_op jit(solution)/shard_map/ppermute | solution.py:161
  215.1 2.9 %collective-permute-done.31.refs_5_ = bf16[256,2048]{1,0:T(8,128)(2,1)} collective-permute-done((bf16[256,2048]{1,0:T(8,128)(2,1)}, bf16[256,2048]{1,0:T(8,128)(2,1)}, u32[]{:S(2)}, u32[]{:S(2)}) %collective-permute-start.31) | collective-permute-done | bytes 1048608 | tf_op jit(solution)/shard_map/ppermute | solution.py:161
  217.9 10.6 %far_rows.1 = (f32[1024,512]{1,0:T(8,128)}, f32[1024,512]{1,0:T(8,128)}) custom-call(s32[2]{0:T(128)} %pad_add_fusion.place, bf16[256,2048]{1,0:T(8,128)(2,1)} %stack.25.refs_0_, bf16[256,2048]{1,0:T(8,128)(2,1)} %stack.26.refs_1_, bf16[256,2048]{1,0:T(8,128)(2,1)} %copy-done.8, ...), custom_call_target="tpu_custom_call", output_to_operand_aliasing={{0}: (9, {}), {1}: (10, {})} | custom-call | tf_op jit(solution)/shard_map/far_rows/pallas_call | solution.py:317
  (110 shorter events, 53.5 us)
Async XLA Ops:
  7.2 188.8 %all-gather.3.cloned.1.call-start = ((), (), s32[]{:S(2)}) async-start(), calls=%async_computation | async-start | bytes 4718592 | tf_op jit(solution)/shard_map/all_gather | solution.py:370
  13.8 17.5 %collective-permute-start.2 = (bf16[1024,128]{1,0:T(8,128)(2,1)}, bf16[1024,128]{1,0:T(8,128)(2,1)S(1)}, u32[]{:S(2)}, u32[]{:S(2)}) collective-permute-start(bf16[1024,128]{1,0:T(8,128)(2,1)} %get-tuple-element.45), channel_id=1, source_target_pairs={{0,4},{2,6},{4,0},{6,2},{1,5},{3,7},{5,1},{7,3},{8,12},{10,14},{12... | collective-permute-start | bytes 786440 | tf_op jit(solution)/shard_map/ppermute | solution.py:161
  15.5 19.4 %collective-permute-start.3 = (bf16[1024,128]{1,0:T(8,128)(2,1)}, bf16[1024,128]{1,0:T(8,128)(2,1)S(1)}, u32[]{:S(2)}, u32[]{:S(2)}) collective-permute-start(bf16[1024,128]{1,0:T(8,128)(2,1)} %get-tuple-element.40.refs_0_), channel_id=1, source_target_pairs={{0,8},{8,0},{1,9},{9,1},{2,10},{10,2},{3,11},{11,3},{4,12},{12,4},... | collective-permute-start | bytes 786440 | tf_op jit(solution)/shard_map/ppermute | solution.py:161
  72.5 15.1 %collective-permute-start.14 = (bf16[128,2048]{1,0:T(8,128)(2,1)}, bf16[128,2048]{1,0:T(8,128)(2,1)}, u32[]{:S(2)}, u32[]{:S(2)}) collective-permute-start(bf16[128,2048]{1,0:T(8,128)(2,1)} %get-tuple-element.54.refs_0_), channel_id=1, source_target_pairs={{0,0},{2,34},{4,68},{6,102},{8,8},{10,42},{12,76},{14,110},{16,80}... | collective-permute-start | bytes 1572872 | tf_op jit(solution)/shard_map/ppermute | solution.py:357
  85.5 15.0 %collective-permute-start.18 = (bf16[128,2048]{1,0:T(8,128)(2,1)S(1)}, bf16[128,2048]{1,0:T(8,128)(2,1)S(1)}, u32[]{:S(2)}, u32[]{:S(2)}) collective-permute-start(bf16[128,2048]{1,0:T(8,128)(2,1)S(1)} %add_convert_fusion.refs_0_), channel_id=1, source_target_pairs={{0,8},{1,9},{8,0},{9,1},{2,10},{3,11},{10,2},{11,3},{4,12},{5,13},... | collective-permute-start | bytes 1572872 | tf_op jit(solution)/shard_map/ppermute | solution.py:161
  86.2 20.0 %collective-permute-start.16 = (bf16[128,2048]{1,0:T(8,128)(2,1)S(1)}, bf16[128,2048]{1,0:T(8,128)(2,1)S(1)}, u32[]{:S(2)}, u32[]{:S(2)}) collective-permute-start(bf16[128,2048]{1,0:T(8,128)(2,1)S(1)} %add_convert_fusion.refs_0_), channel_id=1, source_target_pairs={{0,1},{1,8},{8,9},{9,0},{2,3},{3,10},{10,11},{11,2},{4,5},{5,12},{... | collective-permute-start | bytes 1572872 | tf_op jit(solution)/shard_map/ppermute | solution.py:161
  87.5 34.8 %collective-permute-start.11 = (bf16[128,2048]{1,0:T(8,128)(2,1)}, bf16[128,2048]{1,0:T(8,128)(2,1)}, u32[]{:S(2)}, u32[]{:S(2)}) collective-permute-start(bf16[128,2048]{1,0:T(8,128)(2,1)} %get-tuple-element.54.refs_0_), channel_id=1, source_target_pairs={{0,6},{2,0},{4,2},{6,4},{1,7},{3,1},{5,3},{7,5},{8,14},{10,8},{12,... | collective-permute-start | bytes 1572872 | tf_op jit(solution)/shard_map/ppermute | solution.py:161
  91.6 27.7 %collective-permute-start.17 = (bf16[128,2048]{1,0:T(8,128)(2,1)S(1)}, bf16[128,2048]{1,0:T(8,128)(2,1)S(1)}, u32[]{:S(2)}, u32[]{:S(2)}) collective-permute-start(bf16[128,2048]{1,0:T(8,128)(2,1)S(1)} %add_convert_fusion.refs_0_), channel_id=1, source_target_pairs={{0,9},{1,0},{8,1},{9,8},{2,11},{3,2},{10,3},{11,10},{4,13},{5,4},{... | collective-permute-start | bytes 1572872 | tf_op jit(solution)/shard_map/ppermute | solution.py:161
  94.2 28.1 %collective-permute-start.13 = (bf16[128,2048]{1,0:T(8,128)(2,1)}, bf16[128,2048]{1,0:T(8,128)(2,1)}, u32[]{:S(2)}, u32[]{:S(2)}) collective-permute-start(bf16[128,2048]{1,0:T(8,128)(2,1)} %get-tuple-element.54.refs_0_), channel_id=1, source_target_pairs={{0,4},{2,6},{4,0},{6,2},{1,5},{3,7},{5,1},{7,3},{8,12},{10,14},{12... | collective-permute-start | bytes 1572872 | tf_op jit(solution)/shard_map/ppermute | solution.py:161
  100.6 24.2 %collective-permute-start.15 = (bf16[128,2048]{1,0:T(8,128)(2,1)}, bf16[128,2048]{1,0:T(8,128)(2,1)}, u32[]{:S(2)}, u32[]{:S(2)}) collective-permute-start(bf16[128,2048]{1,0:T(8,128)(2,1)} %collective-permute-done.14), channel_id=1, source_target_pairs={{0,0},{34,32},{68,64},{102,96},{8,16},{42,48},{76,80},{110,112},{8... | collective-permute-start | bytes 1572872 | tf_op jit(solution)/shard_map/ppermute | solution.py:364
  106.2 24.2 %collective-permute-start.20 = (bf16[128,2048]{1,0:T(8,128)(2,1)}, bf16[128,2048]{1,0:T(8,128)(2,1)}, u32[]{:S(2)}, u32[]{:S(2)}) collective-permute-start(bf16[128,2048]{1,0:T(8,128)(2,1)} %collective-permute-done.19), channel_id=1, source_target_pairs={{0,0},{34,32},{68,64},{102,96},{8,16},{42,48},{76,80},{110,112},{8... | collective-permute-start | bytes 1572872 | tf_op jit(solution)/shard_map/ppermute | solution.py:361
  130.4 67.1 %all-gather.5.cloned.1.call-start = ((), (), s32[]{:S(2)}) async-start(), calls=%async_computation.1 | async-start | bytes 4718592 | tf_op jit(solution)/shard_map/all_gather | solution.py:371
  131.2 22.6 %collective-permute-start.22 = (bf16[256,2048]{1,0:T(8,128)(2,1)S(1)}, bf16[256,2048]{1,0:T(8,128)(2,1)S(1)}, u32[]{:S(2)}, u32[]{:S(2)}) collective-permute-start(bf16[256,2048]{1,0:T(8,128)(2,1)S(1)} %copy-done), channel_id=1, source_target_pairs={{0,9},{1,0},{8,1},{9,8},{2,11},{3,2},{10,3},{11,10},{4,13},{5,4},{... | collective-permute-start | bytes 3145736 | tf_op jit(solution)/shard_map/ppermute | solution.py:161
  131.3 26.8 %collective-permute-start.21 = (bf16[256,2048]{1,0:T(8,128)(2,1)S(1)}, bf16[256,2048]{1,0:T(8,128)(2,1)}, u32[]{:S(2)}, u32[]{:S(2)}) collective-permute-start(bf16[256,2048]{1,0:T(8,128)(2,1)S(1)} %copy-done), channel_id=1, source_target_pairs={{0,1},{1,8},{8,9},{9,0},{2,3},{3,10},{10,11},{11,2},{4,5},{5,12},{... | collective-permute-start | bytes 3145736 | tf_op jit(solution)/shard_map/ppermute | solution.py:161
  133.3 24.8 %collective-permute-start.24 = (bf16[256,2048]{1,0:T(8,128)(2,1)S(1)}, bf16[256,2048]{1,0:T(8,128)(2,1)S(1)}, u32[]{:S(2)}, u32[]{:S(2)}) collective-permute-start(bf16[256,2048]{1,0:T(8,128)(2,1)S(1)} %copy-done.1), channel_id=1, source_target_pairs={{0,6},{2,0},{4,2},{6,4},{1,7},{3,1},{5,3},{7,5},{8,14},{10,8},{12,... | collective-permute-start | bytes 3145736 | tf_op jit(solution)/shard_map/ppermute | solution.py:161
  133.3 25.5 %collective-permute-start.23 = (bf16[256,2048]{1,0:T(8,128)(2,1)S(1)}, bf16[256,2048]{1,0:T(8,128)(2,1)}, u32[]{:S(2)}, u32[]{:S(2)}) collective-permute-start(bf16[256,2048]{1,0:T(8,128)(2,1)S(1)} %copy-done.1), channel_id=1, source_target_pairs={{0,2},{2,4},{4,6},{6,0},{1,3},{3,5},{5,7},{7,1},{8,10},{10,12},{12... | collective-permute-start | bytes 3145736 | tf_op jit(solution)/shard_map/ppermute | solution.py:161
  158.8 25.5 %collective-permute-start.26 = (bf16[256,2048]{1,0:T(8,128)(2,1)}, bf16[256,2048]{1,0:T(8,128)(2,1)S(1)}, u32[]{:S(2)}, u32[]{:S(2)}) collective-permute-start(bf16[256,2048]{1,0:T(8,128)(2,1)} %stack.26.refs_1_), channel_id=1, source_target_pairs={{0,9},{1,0},{8,1},{9,8},{2,11},{3,2},{10,3},{11,10},{4,13},{5,4},{... | collective-permute-start | bytes 3145736 | tf_op jit(solution)/shard_map/ppermute | solution.py:161
  160.3 26.5 %collective-permute-start.25 = (bf16[256,2048]{1,0:T(8,128)(2,1)}, bf16[256,2048]{1,0:T(8,128)(2,1)S(1)}, u32[]{:S(2)}, u32[]{:S(2)}) collective-permute-start(bf16[256,2048]{1,0:T(8,128)(2,1)} %stack.26.refs_1_), channel_id=1, source_target_pairs={{0,1},{1,8},{8,9},{9,0},{2,3},{3,10},{10,11},{11,2},{4,5},{5,12},{... | collective-permute-start | bytes 3145736 | tf_op jit(solution)/shard_map/ppermute | solution.py:161
  160.8 26.5 %collective-permute-start.28 = (bf16[256,2048]{1,0:T(8,128)(2,1)S(1)}, bf16[256,2048]{1,0:T(8,128)(2,1)S(1)}, u32[]{:S(2)}, u32[]{:S(2)}) collective-permute-start(bf16[256,2048]{1,0:T(8,128)(2,1)S(1)} %copy-done.2), channel_id=1, source_target_pairs={{0,6},{2,0},{4,2},{6,4},{1,7},{3,1},{5,3},{7,5},{8,14},{10,8},{12,... | collective-permute-start | bytes 3145736 | tf_op jit(solution)/shard_map/ppermute | solution.py:161
  163.0 25.9 %collective-permute-start.27 = (bf16[256,2048]{1,0:T(8,128)(2,1)S(1)}, bf16[256,2048]{1,0:T(8,128)(2,1)S(1)}, u32[]{:S(2)}, u32[]{:S(2)}) collective-permute-start(bf16[256,2048]{1,0:T(8,128)(2,1)S(1)} %copy-done.2), channel_id=1, source_target_pairs={{0,2},{2,4},{4,6},{6,0},{1,3},{3,5},{5,7},{7,1},{8,10},{10,12},{12... | collective-permute-start | bytes 3145736 | tf_op jit(solution)/shard_map/ppermute | solution.py:161
  188.9 26.1 %collective-permute-start.29 = (bf16[256,2048]{1,0:T(8,128)(2,1)}, bf16[256,2048]{1,0:T(8,128)(2,1)S(1)}, u32[]{:S(2)}, u32[]{:S(2)}) collective-permute-start(bf16[256,2048]{1,0:T(8,128)(2,1)} %collective-permute-done.21.refs_0_), channel_id=1, source_target_pairs={{0,1},{1,8},{8,9},{9,0},{2,3},{3,10},{10,11},{11,2},{4,5},{5,12},{... | collective-permute-start | bytes 3145736 | tf_op jit(solution)/shard_map/ppermute | solution.py:161
  189.2 25.9 %collective-permute-start.30 = (bf16[256,2048]{1,0:T(8,128)(2,1)S(1)}, bf16[256,2048]{1,0:T(8,128)(2,1)}, u32[]{:S(2)}, u32[]{:S(2)}) collective-permute-start(bf16[256,2048]{1,0:T(8,128)(2,1)S(1)} %collective-permute-done.26.refs_3_), channel_id=1, source_target_pairs={{0,9},{1,0},{8,1},{9,8},{2,11},{3,2},{10,3},{11,10},{4,13},{5,4},{... | collective-permute-start | bytes 3145736 | tf_op jit(solution)/shard_map/ppermute | solution.py:161
  192.1 25.8 %collective-permute-start.31 = (bf16[256,2048]{1,0:T(8,128)(2,1)}, bf16[256,2048]{1,0:T(8,128)(2,1)}, u32[]{:S(2)}, u32[]{:S(2)}) collective-permute-start(bf16[256,2048]{1,0:T(8,128)(2,1)} %collective-permute-done.23.refs_7_), channel_id=1, source_target_pairs={{0,2},{2,4},{4,6},{6,0},{1,3},{3,5},{5,7},{7,1},{8,10},{10,12},{12... | collective-permute-start | bytes 3145736 | tf_op jit(solution)/shard_map/ppermute | solution.py:161
  192.3 25.6 %collective-permute-start.32 = (bf16[256,2048]{1,0:T(8,128)(2,1)S(1)}, bf16[256,2048]{1,0:T(8,128)(2,1)}, u32[]{:S(2)}, u32[]{:S(2)}) collective-permute-start(bf16[256,2048]{1,0:T(8,128)(2,1)S(1)} %collective-permute-done.28.refs_10_), channel_id=1, source_target_pairs={{0,6},{2,0},{4,2},{6,4},{1,7},{3,1},{5,3},{7,5},{8,14},{10,8},{12,... | collective-permute-start | bytes 3145736 | tf_op jit(solution)/shard_map/ppermute | solution.py:161
  (36 other events, 465.6 us)
Sparse Core Ops, SparseCore 0:
  130.6 33.0 all-gather.2
  165.4 32.0 all-gather.4
